TPU v7x, 256 devices: a whole 4x4x8 slice. The times are simulated.
256 devices in a mesh: ty: 8 (over z_hi, x), tx: 32 (over z_lo, y, core).
Axes of the slice: x: 4, y: 4, z: 8 (z_hi: 2, z_lo: 4; z = z_hi * 4 + z_lo), core: 2. Of those that a mesh axis runs over, the one named last changes fastest.
Arguments:
- object_field: float32 [2, 1024, 4096], P(None, 'ty', 'tx'), may hold values from -40 to 40
- probe: float32 [2, 4, 128, 128], replicated, may hold values from -3 to 3
- intensities: float32 [8, 32, 3, 128, 128], P('ty', 'tx'), may hold values from 0.25 to 16
- positions: int32 [8, 32, 3, 2], P('ty', 'tx'), may hold values from 0 to 128
Outputs:
- object_out: float32 [2, 1024, 4096], P(None, 'ty', 'tx')
- probe_out: float32 [2, 4, 128, 128], replicated
All inputs are finite; a program needn't handle non-finite values.
Results may differ from a plain program's by a relative error of at most 0.0003.
Values sent between devices are 32-bit elements; how exact they have to be, the bound alone decides.
A program may use at most 64 MiB of HBM per device.

v0:
```python
import jax
import jax.numpy as jnp
from jax import lax
from jax.sharding import PartitionSpec as P

ROUNDS = 2


OBJECT_STEP = 0.1
PROBE_RELAX = 0.5


def padded_2(x, sides, width):
    for axis, dim in sides:
        size, length = (lax.axis_size(axis), x.shape[dim])
        up = [(i, (i + 1) % size) for i in range(size - 1)]
        down = [(j, i) for i, j in up]
        last = lax.slice_in_dim(x, length - width, length, axis=dim)
        initial = lax.slice_in_dim(x, 0, width, axis=dim)
        before = lax.ppermute(last, axis, up)
        after = lax.ppermute(initial, axis, down)
        x = jnp.concatenate([before, x, after], axis=dim)
    return x


def dft_tables(win_size):
    index_line = jnp.arange(win_size, dtype=jnp.int32)
    product = index_line[:, None] * index_line[None, :] % win_size
    angle = product.astype(jnp.float32) * (2.0 * jnp.pi / win_size)
    scaling = win_size ** (-0.5)
    return (jnp.cos(angle) * scaling, jnp.sin(angle) * scaling)


def transform(part_re, part_im, cosine_table, sine_table, flip_sign):
    exact = lax.Precision.HIGHEST
    c_re = jnp.einsum("ux,bxy->buy", cosine_table, part_re, precision=exact)
    c_im = jnp.einsum("ux,bxy->buy", cosine_table, part_im, precision=exact)
    s_re = jnp.einsum("ux,bxy->buy", sine_table, part_re, precision=exact)
    s_im = jnp.einsum("ux,bxy->buy", sine_table, part_im, precision=exact)
    mid_re = c_re - flip_sign * s_im
    mid_im = c_im + flip_sign * s_re
    c_re = jnp.einsum("bxy,vy->bxv", mid_re, cosine_table, precision=exact)
    c_im = jnp.einsum("bxy,vy->bxv", mid_im, cosine_table, precision=exact)
    s_re = jnp.einsum("bxy,vy->bxv", mid_re, sine_table, precision=exact)
    s_im = jnp.einsum("bxy,vy->bxv", mid_im, sine_table, precision=exact)
    return (c_re - flip_sign * s_im, c_im + flip_sign * s_re)


def fold_rims(padded, axis_dim, tile_size, margin):
    upper_rim = lax.slice_in_dim(padded, 0, margin, axis=axis_dim)
    middle = lax.slice_in_dim(padded, 2 * margin, 2 * margin + tile_size, axis=axis_dim)
    lower_rim = lax.slice_in_dim(
        padded, tile_size + 3 * margin, tile_size + 4 * margin, axis=axis_dim
    )
    first_part = lax.slice_in_dim(middle, 0, margin, axis=axis_dim) + upper_rim
    centre = lax.slice_in_dim(middle, margin, tile_size - margin, axis=axis_dim)
    last_part = lax.slice_in_dim(middle, tile_size - margin, tile_size, axis=axis_dim) + lower_rim
    return jnp.concatenate([first_part, centre, last_part], axis=axis_dim)


def per_device(object_field, probe, intensities, positions):
    win_size = probe.shape[-1]
    margin = win_size // 2
    tile_size = object_field.shape[-1]
    mode_count = probe.shape[1]
    scan_count = positions.shape[2]
    scan_spots = positions.reshape(scan_count, 2)
    measured = jnp.sqrt(intensities.reshape(scan_count, win_size, win_size))
    cosine_table, sine_table = dft_tables(win_size)
    zero_index = jnp.zeros((), jnp.int32)
    for round_index in range(ROUNDS):
        extended = padded_2(object_field, (("ty", 1), ("tx", 2)), margin)

        def cut_window(corner):
            return lax.dynamic_slice(
                extended, (zero_index, corner[0], corner[1]), (2, win_size, win_size)
            )

        windows = jax.vmap(cut_window)(scan_spots)
        win_re = windows[:, 0][:, None]
        win_im = windows[:, 1][:, None]
        probe_re = probe[0][None]
        probe_im = probe[1][None]
        batch_shape = (scan_count * mode_count, win_size, win_size)
        split_shape = (scan_count, mode_count, win_size, win_size)
        wave_re = (probe_re * win_re - probe_im * win_im).reshape(batch_shape)
        wave_im = (probe_re * win_im + probe_im * win_re).reshape(batch_shape)
        far_re, far_im = transform(wave_re, wave_im, cosine_table, sine_table, -1.0)
        far_re = far_re.reshape(split_shape)
        far_im = far_im.reshape(split_shape)
        far_power = jnp.sum(far_re * far_re + far_im * far_im, axis=1)
        factor = (measured / jnp.sqrt(jnp.maximum(far_power, 1.0)) - 1.0)[:, None]
        diff_re = (far_re * factor).reshape(batch_shape)
        diff_im = (far_im * factor).reshape(batch_shape)
        back_re, back_im = transform(diff_re, diff_im, cosine_table, sine_table, 1.0)
        back_re = back_re.reshape(split_shape)
        back_im = back_im.reshape(split_shape)
        grad_re = jnp.sum(probe_re * back_re + probe_im * back_im, axis=1)
        grad_im = jnp.sum(probe_re * back_im - probe_im * back_re, axis=1)
        probe_grad = jnp.stack(
            [
                jnp.sum(win_re * back_re + win_im * back_im, axis=0),
                jnp.sum(win_re * back_im - win_im * back_re, axis=0),
            ]
        )
        weight = jnp.sum(windows * windows)

        def place(scan_index, grid_now):
            corner = scan_spots[scan_index]
            start_tuple = (zero_index, corner[0], corner[1])
            previous = lax.dynamic_slice(grid_now, start_tuple, (2, win_size, win_size))
            grad_piece = jnp.stack([grad_re[scan_index], grad_im[scan_index]])
            return lax.dynamic_update_slice(grid_now, previous + grad_piece, start_tuple)

        grad_grid = lax.fori_loop(0, scan_count, place, jnp.zeros_like(extended))
        widened = padded_2(grad_grid, (("ty", 1), ("tx", 2)), margin)
        update = fold_rims(fold_rims(widened, 1, tile_size, margin), 2, tile_size, margin)
        new_object = object_field + OBJECT_STEP * update
        grad_total, weight_all = lax.psum((probe_grad, weight), ("ty", "tx"))
        probe = probe + PROBE_RELAX * win_size * win_size / weight_all * grad_total
        object_field = new_object
    return (object_field, probe)


def solution(mesh):
    placed = (P(None, "ty", "tx"), P(), P("ty", "tx", None, None, None), P("ty", "tx", None, None))
    return jax.shard_map(
        per_device,
        mesh=mesh,
        in_specs=placed,
        out_specs=(P(None, "ty", "tx"), P()),
        check_vma=False,
    )
```

profile of v0, /device:TPU:1, one launch (start us, length us, event | category | flops | bytes accessed | tf_op | source)
XLA Modules:
  0.0 733.4 jit_solution(17040615046503731448)
XLA Ops:
  8.1 4.1 collective-permute-start
  13.7 3.5 collective-permute-done.1
  17.4 5.3 collective-permute-start.2
  22.7 1.9 collective-permute-start.3
  26.0 4.4 collective-permute-done.3
  30.7 6.2 while.30
  37.6 1.5 convolution_multiply_fusion.7
  39.1 1.5 convolution_multiply_fusion.6
  40.7 1.5 fusion.7
  42.2 1.5 fusion.6
  43.7 1.5 convolution_multiply_fusion.5
  45.2 1.5 convolution_multiply_fusion.4
  46.8 1.5 convolution_subtract_fusion.6
  48.3 1.8 multiply_add_fusion.2
  52.0 1.5 fusion.61
  53.6 1.5 fusion.57
  55.1 1.5 fusion.5
  56.6 1.5 fusion.59
  58.2 1.5 fusion.4
  61.2 1.5 convolution_subtract_fusion.4
  62.8 13.8 %convolution_add_fusion.4 = f32[12,128,128]{2,1,0:T(8,128)S(1)} fusion(f32[12,128,128]{2,1,0:T(8,128)S(1)} %fusion.55, f32[12,128,128]{1,2,0:T(8,128)S(1)} %fusion.5), kind=kOutput, calls=%fused_computation.28 | convolution fusion | flops 302432256 | bytes 2359296 | tf_op jit(solution)/shard_map/bxy,vy->bxv/dot_general | solution.py:44
  77.1 21.3 %while.28 = (s32[]{:T(128)}, f32[2,256,256]{2,1,0:T(8,128)S(1)}, s32[3,2]{0,1:T(2,128)S(1)}, f32[3,128,128]{2,1,0:T(8,128)S(1)}, f32[3,128,128]{2,1,0:T(8,128)S(1)}, /*index=5*/s32[]{:T(128)}, s32[]{:T(128)}, s32[]{:T(128)}) while((s32[]{:T(128)}, f32[2,256,256]{2,1,0:T(8,128)S(1)}, s32[3,2]{0,1:T(2,128)S(1)}, f32[3,128,128]{2,1,0:T(8,128)S(1)}, ...), condition=%wide.region_4.5_spmd, body=%wide.region_3.4_spmd.sunk | while | flops 65544 | bytes 917709 | solution.py:115
  81.9 2.4 dynamic_update_slice.16
  89.2 2.2 dynamic_update_slice.16
  96.3 2.1 dynamic_update_slice.16
  98.4 3.2 collective-permute-start.4
  103.7 8.4 %collective-permute-done.5 = f32[2,64,256]{2,1,0:T(8,128)S(1)} collective-permute-done((f32[2,64,256]{2,1,0:T(8,128)S(1)}, f32[2,64,256]{2,1,0:T(8,128)S(1)}, u32[]{:S(2)}, u32[]{:S(2)}) %collective-permute-start.5) | collective-permute-done | bytes 131104 | tf_op jit(solution)/shard_map/ppermute | solution.py:21
  112.3 3.1 collective-permute-start.6
  115.4 1.9 collective-permute-start.7
  117.4 2.8 collective-permute-done.6
  120.1 4.4 collective-permute-done.7
  125.9 10.5 %collective-permute-start.8 = (f32[2,64,128]{2,1,0:T(8,128)S(1)}, f32[2,64,128]{2,1,0:T(8,128)S(1)}, u32[]{:S(2)}, u32[]{:S(2)}) collective-permute-start(f32[2,64,128]{2,1,0:T(8,128)S(1)} %get-tuple-element.314), channel_id=1, source_target_pairs={{0,32},{32,64},{64,96},{96,128},{128,160},{160,192},{192,224},{1,3... | collective-permute-start | bytes 196616 | tf_op jit(solution)/shard_map/ppermute | solution.py:20
  137.7 4.3 collective-permute-done.9
  142.1 3.5 collective-permute-start.10
  145.6 1.9 collective-permute-start.11
  148.9 4.4 collective-permute-done.11
  153.6 6.3 while.31
  160.7 93.4 %all-reduce = (f32[]{:T(128)}, f32[]{:T(128)}) all-reduce(f32[]{:T(128)} %get-tuple-element.325, f32[]{:T(128)} %get-tuple-element.324), channel_id=1, replica_groups=mesh['ty'=8,'tx'=32] {'ty','tx'}, use_global_device_ids=true, to_apply=%region_6.7 | all-reduce | flops 2 | bytes 16 | tf_op jit(solution)/shard_map/psum | solution.py:119
  254.8 159.8 %all-reduce.4.cloned.1.call-done = f32[2,4,128,128]{3,2,1,0:T(8,128)} async-done(((f32[2,4,128,128]{3,2,1,0:T(8,128)}), f32[2,4,128,128]{3,2,1,0:T(8,128)}) %all-reduce.4.cloned.1.call-update) | async-done | bytes 524304 | tf_op jit(solution)/shard_map/psum | solution.py:119
  416.0 1.5 convolution_multiply_fusion.3
  417.5 1.5 convolution_multiply_fusion.2
  419.0 1.5 fusion.3
  420.6 1.5 convolution_multiply_fusion
  422.1 1.5 fusion.2
  423.6 1.5 convolution_multiply_fusion.1
  425.1 1.5 convolution_subtract_fusion.2
  426.7 1.7 multiply_add_fusion
  430.4 1.5 fusion.49
  431.9 1.5 fusion.45
  433.4 1.5 fusion.1
  436.5 1.5 fusion
  438.0 1.5 fusion.43
  439.6 1.5 convolution_subtract_fusion
  441.4 1.5 convolution_add_fusion
  443.4 21.3 %while.29 = (s32[]{:T(128)}, f32[2,256,256]{2,1,0:T(8,128)S(1)}, s32[3,2]{0,1:T(2,128)S(1)}, f32[3,128,128]{2,1,0:T(8,128)S(1)}, f32[3,128,128]{2,1,0:T(8,128)S(1)}, /*index=5*/s32[]{:T(128)}, s32[]{:T(128)}, s32[]{:T(128)}) while((s32[]{:T(128)}, f32[2,256,256]{2,1,0:T(8,128)S(1)}, s32[3,2]{0,1:T(2,128)S(1)}, ...), condition=%wide.region_14.15_spmd, body=%wide.region_13.14_spmd.sunk | while | flops 65544 | bytes 917709 | solution.py:115
  448.3 2.4 dynamic_update_slice.17
  455.5 2.2 dynamic_update_slice.17
  462.6 2.1 dynamic_update_slice.17
  464.8 3.2 collective-permute-start.12
  470.9 4.3 collective-permute-done.13
  475.4 6.5 collective-permute-start.14
  481.9 1.9 collective-permute-start.15
  483.9 239.1 %all-reduce.6.cloned.1.call-done = f32[2,4,128,128]{3,2,1,0:T(8,128)} async-done(((f32[2,4,128,128]{3,2,1,0:T(8,128)}), f32[2,4,128,128]{3,2,1,0:T(8,128)}) %all-reduce.6.cloned.1.call-update) | async-done | bytes 524304 | tf_op jit(solution)/shard_map/psum | solution.py:119
  723.0 1.9 multiply_add_fusion.4
  (134 shorter events, 42.2 us)
Async XLA Ops:
  7.2 407.4 %all-reduce.4.cloned.1.call-start = ((), (), s32[]{:S(2)}) async-start(), calls=%async_computation | async-start | bytes 1048576 | tf_op jit(solution)/shard_map/psum | solution.py:119
  7.2 6.3 copy-start.10
  8.1 5.5 copy-start.8
  8.1 5.5 collective-permute-start
  12.2 5.0 collective-permute-start.1
  17.2 7.4 %copy-start = (f32[2,4,128,128]{3,2,1,0:T(8,128)S(1)}, f32[2,4,128,128]{3,2,1,0:T(8,128)}, u32[]{:S(2)}) copy-start(f32[2,4,128,128]{3,2,1,0:T(8,128)} %param.9) | copy-start | bytes 1572868
  17.4 8.6 %collective-permute-start.2 = (f32[2,256,64]{2,1,0:T(8,128)S(1)}, f32[2,256,64]{2,1,0:T(8,128)S(1)}, u32[]{:S(2)}, u32[]{:S(2)}) collective-permute-start(f32[2,256,64]{2,1,0:T(8,128)S(1)} %get-tuple-element.308), channel_id=1, source_target_pairs={{0,1},{1,2},{2,3},{3,4},{4,5},{5,6},{6,7},{7,8},{8,9},{9,10},{10,1... | collective-permute-start | bytes 393224 | tf_op jit(solution)/shard_map/ppermute | solution.py:20
  22.7 7.7 %collective-permute-start.3 = (f32[2,256,64]{2,1,0:T(8,128)S(1)}, f32[2,256,64]{2,1,0:T(8,128)S(1)}, u32[]{:S(2)}, u32[]{:S(2)}) collective-permute-start(f32[2,256,64]{2,1,0:T(8,128)S(1)} %get-tuple-element.309), channel_id=1, source_target_pairs={{1,0},{2,1},{3,2},{4,3},{5,4},{6,5},{7,6},{8,7},{9,8},{10,9},{11,1... | collective-permute-start | bytes 393224 | tf_op jit(solution)/shard_map/ppermute | solution.py:21
  36.9 0.7 copy-start.6
  62.8 13.8 %copy-start.7 = (f32[3,128,128]{2,1,0:T(8,128)S(1)}, f32[3,128,128]{2,1,0:T(8,128)}, u32[]{:S(2)}) copy-start(f32[3,128,128]{2,1,0:T(8,128)} %copy-done.6) | copy-start | bytes 589828
  98.4 5.2 collective-permute-start.4
  101.7 10.4 %collective-permute-start.5 = (f32[2,64,256]{2,1,0:T(8,128)S(1)}, f32[2,64,256]{2,1,0:T(8,128)S(1)}, u32[]{:S(2)}, u32[]{:S(2)}) collective-permute-start(f32[2,64,256]{2,1,0:T(8,128)S(1)} %get-tuple-element.294), channel_id=1, source_target_pairs={{32,0},{64,32},{96,64},{128,96},{160,128},{192,160},{224,192},{33,... | collective-permute-start | bytes 393224 | tf_op jit(solution)/shard_map/ppermute | solution.py:21
  112.3 7.8 %collective-permute-start.6 = (f32[2,384,64]{2,1,0:T(8,128)S(1)}, f32[2,384,64]{2,1,0:T(8,128)S(1)}, u32[]{:S(2)}, u32[]{:S(2)}) collective-permute-start(f32[2,384,64]{2,1,0:T(8,128)S(1)} %get-tuple-element.288), channel_id=1, source_target_pairs={{0,1},{1,2},{2,3},{3,4},{4,5},{5,6},{6,7},{7,8},{8,9},{9,10},{10,1... | collective-permute-start | bytes 589832 | tf_op jit(solution)/shard_map/ppermute | solution.py:20
  115.4 9.1 %collective-permute-start.7 = (f32[2,384,64]{2,1,0:T(8,128)S(1)}, f32[2,384,64]{2,1,0:T(8,128)S(1)}, u32[]{:S(2)}, u32[]{:S(2)}) collective-permute-start(f32[2,384,64]{2,1,0:T(8,128)S(1)} %get-tuple-element.289), channel_id=1, source_target_pairs={{1,0},{2,1},{3,2},{4,3},{5,4},{6,5},{7,6},{8,7},{9,8},{10,9},{11,1... | collective-permute-start | bytes 589832 | tf_op jit(solution)/shard_map/ppermute | solution.py:21
  124.9 0.9 copy-start.9
  125.9 11.8 %collective-permute-start.8 = (f32[2,64,128]{2,1,0:T(8,128)S(1)}, f32[2,64,128]{2,1,0:T(8,128)S(1)}, u32[]{:S(2)}, u32[]{:S(2)}) collective-permute-start(f32[2,64,128]{2,1,0:T(8,128)S(1)} %get-tuple-element.314), channel_id=1, source_target_pairs={{0,32},{32,64},{64,96},{96,128},{128,160},{160,192},{192,224},{1,3... | collective-permute-start | bytes 196616 | tf_op jit(solution)/shard_map/ppermute | solution.py:20
  136.4 5.6 collective-permute-start.9
  142.1 6.8 collective-permute-start.10
  145.6 7.7 %collective-permute-start.11 = (f32[2,256,64]{2,1,0:T(8,128)S(1)}, f32[2,256,64]{2,1,0:T(8,128)S(1)}, u32[]{:S(2)}, u32[]{:S(2)}) collective-permute-start(f32[2,256,64]{2,1,0:T(8,128)S(1)} %get-tuple-element.307), channel_id=1, source_target_pairs={{1,0},{2,1},{3,2},{4,3},{5,4},{6,5},{7,6},{8,7},{9,8},{10,9},{11,1... | collective-permute-start | bytes 393224 | tf_op jit(solution)/shard_map/ppermute | solution.py:21
  148.4 574.5 %all-reduce.6.cloned.1.call-start = ((), (), s32[]{:S(2)}) async-start(), calls=%async_computation.1 | async-start | bytes 1048576 | tf_op jit(solution)/shard_map/psum | solution.py:119
  160.7 253.9 %copy-start.1 = (f32[2,4,128,128]{3,2,1,0:T(8,128)S(1)}, f32[2,4,128,128]{3,2,1,0:T(8,128)}, u32[]{:S(2)}) copy-start(f32[2,4,128,128]{3,2,1,0:T(8,128)} %param.9) | copy-start | bytes 1572868
  254.8 161.0 %copy-start.2 = (f32[3,128,128]{2,1,0:T(8,128)}, f32[3,128,128]{2,1,0:T(8,128)S(1)}, u32[]{:S(2)}) copy-start(f32[3,128,128]{2,1,0:T(8,128)S(1)} %get-tuple-element.300) | copy-start | bytes 589828
  254.8 161.0 %copy-start.4 = (f32[3,128,128]{2,1,0:T(8,128)}, f32[3,128,128]{2,1,0:T(8,128)S(1)}, u32[]{:S(2)}) copy-start(f32[3,128,128]{2,1,0:T(8,128)S(1)} %get-tuple-element.301) | copy-start | bytes 589828
  441.1 1.8 copy-start.3
  441.1 1.8 copy-start.5
  464.8 6.1 collective-permute-start.12
  469.5 5.7 collective-permute-start.13
  475.4 249.4 %collective-permute-start.14 = (f32[2,384,64]{2,1,0:T(8,128)S(1)}, f32[2,384,64]{2,1,0:T(8,128)S(1)}, u32[]{:S(2)}, u32[]{:S(2)}) collective-permute-start(f32[2,384,64]{2,1,0:T(8,128)S(1)} %get-tuple-element.286), channel_id=1, source_target_pairs={{0,1},{1,2},{2,3},{3,4},{4,5},{5,6},{6,7},{7,8},{8,9},{9,10},{10,1... | collective-permute-start | bytes 589832 | tf_op jit(solution)/shard_map/ppermute | solution.py:20
  481.9 242.9 %collective-permute-start.15 = (f32[2,384,64]{2,1,0:T(8,128)S(1)}, f32[2,384,64]{2,1,0:T(8,128)S(1)}, u32[]{:S(2)}, u32[]{:S(2)}) collective-permute-start(f32[2,384,64]{2,1,0:T(8,128)S(1)} %get-tuple-element.287), channel_id=1, source_target_pairs={{1,0},{2,1},{3,2},{4,3},{5,4},{6,5},{7,6},{8,7},{9,8},{10,9},{11,1... | collective-permute-start | bytes 589832 | tf_op jit(solution)/shard_map/ppermute | solution.py:21
Sparse Core Ops, SparseCore 0:
  148.5 266.0 all-reduce.3
  468.9 253.9 all-reduce.5
where the time goes:
time: 744 us; the launch traced here: 733 us
  waiting for transfers between devices  438 us (59%)
  blocking collectives  93.4 us (13%)
  matrix products  61.5 us (8%)
  starting transfers between devices  52.4 us (7%)
  local copies, waits for them, and re-layouts  33.2 us (4%)
  loops' own time  24.5 us (3%)
  between operations  17 us (2%)
  other arithmetic  13.7 us (2%)
    psum x2, waiting for transfers between devices, per_device(): grad_total, weight_all = lax.psum((probe_grad, weight), ('ty', 'tx'))  399 us
    psum x1, blocking collectives, per_device(): grad_total, weight_all = lax.psum((probe_grad, weight), ('ty', 'tx'))  93.4 us
    ppermute x8, starting transfers between devices, padded_2(): before = lax.ppermute(last, axis, up)  39.4 us
    ppermute x8, waiting for transfers between devices, padded_2(): after = lax.ppermute(initial, axis, down)  33.7 us
    another operation x2, loops' own time, per_device(): grad_grid = lax.fori_loop(0, scan_count, place, jnp.zeros_like(extended))  24.3 us
    dot_general x4, matrix products, transform(): s_re = jnp.einsum('bxy,vy->bxv', mid_re, sine_table, precision=exact)  18.4 us
  transfers between devices with their start and end apart: 18, of which 13 were waited for; matrix products, arithmetic and copies ran while one was open for 2% of the time, Pallas kernels for 0%

commit v1 on v0

v1 whole, which is shorter than its diff:
```python
import functools
import jax
import jax.numpy as jnp
import ml_dtypes
import numpy as np
from jax import lax
from jax.experimental import pallas as pl
from jax.experimental.pallas import tpu as pltpu
from jax.sharding import PartitionSpec as P

ROUNDS = 2
OBJECT_STEP = 0.1
PROBE_RELAX = 0.5
WIN = 128
MODES = 4
SCANS = 3
X, Y, ZH, ZL = 4, 4, 2, 4
HALF = MODES * WIN
MESH = pl.DeviceIdType.MESH
F32, BF16 = jnp.float32, jnp.bfloat16


def dft_tables():
    line = np.arange(WIN)
    angle = (line[:, None] * line[None, :] % WIN) * (2.0 * np.pi / WIN)
    c, s = np.cos(angle) * WIN**-0.5, np.sin(angle) * WIN**-0.5
    a = np.block([[c, -s], [s, c]])
    parts = []
    for m in (a, a.T):
        hi = m.astype(ml_dtypes.bfloat16)
        lo = (m - hi.astype(np.float64)).astype(ml_dtypes.bfloat16)
        parts += [hi, lo]
    return np.stack(parts)


def split(x):
    hi = x.astype(BF16)
    return hi, (x - hi.astype(F32)).astype(BF16)


def mm(a, b):
    return jnp.dot(a, b, preferred_element_type=F32)


def kernel(
    obj, probe, inten, pos, tab, obj_out, probe_out,
    ext, zp, gq, lrb, eb, udb, pk, hlr, hud, hco, xh, xl, uf, win, pg, wacc,
    crb, hs, rxb, zbuf, pn, wcb, w1, wxb, wzb,
    halo_s, halo_r, lr_s, lr_r, ud_s, ud_r, co_s, co_r, xy_s, xy_r, z_s, z_r, ag_s, ag_r, fw_s, fw_r,
):
    ty, tx = lax.axis_index("ty"), lax.axis_index("tx")
    nty, ntx = ZH * X, ZL * Y * 2
    zh, x = ty // X, ty % X
    zl, y, core = tx // (2 * Y), (tx // 2) % Y, tx % 2
    z = zh * ZL + zl
    q = x * Y + y
    piece = HALF // (X * Y)
    nz = ZH * ZL

    up, down = (ty + nty - 1) % nty, (ty + 1) % nty
    left, right = (tx + ntx - 1) % ntx, (tx + 1) % ntx
    has_up, has_down = ty > 0, ty < nty - 1
    has_left, has_right = tx > 0, tx < ntx - 1
    partner = (ty, tx + 1 - 2 * core)

    def xy_peer(d):
        px, py = (x + d // Y) % X, (y + d % Y) % Y
        return (zh * X + px, zl * 2 * Y + py * 2 + core), px * Y + py

    def z_peer(d):
        pz = (z + d) % nz
        return ((pz // ZL) * X + x, (pz % ZL) * 2 * Y + y * 2 + core)

    def remote(src, dst, ssem, rsem, device):
        return pltpu.make_async_remote_copy(
            src_ref=src, dst_ref=dst, send_sem=ssem, recv_sem=rsem, device_id=device, device_id_type=MESH
        )

    lane = lax.broadcasted_iota(jnp.int32, (WIN, WIN), 1)
    low = lane < 64
    o_re, o_im = obj[0], obj[1]
    r_re, r_im = pltpu.roll(o_re, 64, 1), pltpu.roll(o_im, 64, 1)
    pk[0] = jnp.where(low, o_re, r_im)
    pk[1] = jnp.where(low, r_re, o_im)

    peers = [partner, (ty, left), (ty, right), (up, tx), (down, tx), (up, left), (up, right), (down, left), (down, right)]
    peers += [xy_peer(d)[0] for d in range(1, X * Y)] + [z_peer(d) for d in range(1, nz)]
    barrier = pltpu.get_barrier_semaphore()
    for peer in peers:
        pl.semaphore_signal(barrier, inc=1, device_id=peer, device_id_type=MESH)
    zp[...] = jnp.zeros_like(zp)
    pl.semaphore_wait(barrier, len(peers))

    top, bottom = pl.ds(0, 64), pl.ds(64, 64)
    halo = [
        (obj.at[:, bottom, :], hud.at[0], (down, tx)),
        (obj.at[:, top, :], hud.at[1], (up, tx)),
        (pk.at[1], hlr.at[0], (ty, right)),
        (pk.at[0], hlr.at[1], (ty, left)),
        (pk.at[1, bottom, :], hco.at[0], (down, right)),
        (pk.at[0, bottom, :], hco.at[1], (down, left)),
        (pk.at[1, top, :], hco.at[2], (up, right)),
        (pk.at[0, top, :], hco.at[3], (up, left)),
    ]
    halo = [remote(s, d, halo_s.at[i], halo_r.at[i], p) for i, (s, d, p) in enumerate(halo)]
    for copy in halo:
        copy.start()
    for copy in halo:
        copy.wait_recv()
    zero = jnp.float32(0.0)

    def extend(rows, mid_re, mid_im, from_left, from_right, keep):
        n = mid_re.shape[0]
        low_n = low[:n]
        keep_l = jnp.where(keep & has_left, 1.0, 0.0)
        keep_r = jnp.where(keep & has_right, 1.0, 0.0)
        keep_m = jnp.where(keep, 1.0, 0.0)
        m_re, m_im = pltpu.roll(mid_re, 64, 1) * keep_m, pltpu.roll(mid_im, 64, 1) * keep_m
        fl, fr = from_left * keep_l, from_right * keep_r
        ext[0, 0, rows, :] = jnp.where(low_n, fl, m_re)
        ext[0, 1, rows, :] = jnp.where(low_n, pltpu.roll(fl, 64, 1), m_im)
        ext[1, 0, rows, :] = jnp.where(low_n, m_re, pltpu.roll(fr, 64, 1))
        ext[1, 1, rows, :] = jnp.where(low_n, m_im, fr)

    extend(pl.ds(64, 128), obj[0], obj[1], hlr[0], hlr[1], True)
    extend(pl.ds(0, 64), hud[0, 0], hud[0, 1], hco[0], hco[1], has_up)
    extend(pl.ds(192, 64), hud[1, 0], hud[1, 1], hco[2], hco[3], has_down)

    for rnd in range(ROUNDS):
        probe_now = probe if rnd == 0 else pn.at[rnd - 1]
        gq[rnd] = jnp.zeros_like(gq.at[rnd])
        pg[rnd] = jnp.zeros_like(pg.at[rnd])
        wacc[rnd] = jnp.zeros_like(wacc.at[rnd])

        def scan(s, carry):
            r, c = pos[s, 0], pos[s, 1]
            back = (WIN - c) & (WIN - 1)
            first = lane + c < WIN
            w = wacc[rnd]
            for comp in range(2):
                x0 = pltpu.roll(ext[0, comp, pl.ds(r, WIN), :], back, 1)
                x1 = pltpu.roll(ext[1, comp, pl.ds(r, WIN), :], back, 1)
                o = jnp.where(first, x0, x1)
                win[comp] = o
                w = w + jnp.sum((o * o).reshape(WIN // 8, 8, WIN), axis=0)
            wacc[rnd] = w
            w_re, w_im = win[0], win[1]
            for k in range(MODES):
                cols = slice(k * WIN, (k + 1) * WIN)
                p_re, p_im = probe_now[cols, :], probe_now[HALF + k * WIN : HALF + (k + 1) * WIN, :]
                xh[0:WIN, cols], xl[0:WIN, cols] = split(p_re * w_re - p_im * w_im)
                xh[WIN:, cols], xl[WIN:, cols] = split(p_re * w_im + p_im * w_re)
            power = jnp.zeros((WIN, WIN), F32)
            for j in range(MODES // 2):
                cols = slice(j * 256, (j + 1) * 256)
                t = mm(tab[2], xh[:, cols]) + mm(tab[2], xl[:, cols]) + mm(tab[3], xh[:, cols])
                for i in range(2):
                    k = 2 * j + i
                    yt = jnp.concatenate([t[0:WIN, i * WIN : (i + 1) * WIN], t[WIN:, i * WIN : (i + 1) * WIN]], axis=1)
                    yh, yl = split(yt)
                    u = mm(yh, tab[0]) + mm(yl, tab[0]) + mm(yh, tab[1])
                    uf[k] = u
                    power = power + u[:, 0:WIN] * u[:, 0:WIN] + u[:, WIN:] * u[:, WIN:]
            factor = jnp.sqrt(inten[s]) / jnp.sqrt(jnp.maximum(power, 1.0)) - 1.0
            factor = jnp.concatenate([factor, factor], axis=1)
            for k in range(MODES):
                cols = slice(k * WIN, (k + 1) * WIN)
                vh, vl = split(uf[k] * factor)
                b = mm(vh, tab[2]) + mm(vl, tab[2]) + mm(vh, tab[3])
                xh[0:WIN, cols], xl[0:WIN, cols] = split(b[:, 0:WIN])
                xh[WIN:, cols], xl[WIN:, cols] = split(b[:, WIN:])
            g_re = jnp.zeros((WIN, WIN), F32)
            g_im = jnp.zeros((WIN, WIN), F32)
            for j in range(MODES // 2):
                cols = slice(j * 256, (j + 1) * 256)
                b = mm(tab[0], xh[:, cols]) + mm(tab[0], xl[:, cols]) + mm(tab[1], xh[:, cols])
                for i in range(2):
                    k = 2 * j + i
                    b_re, b_im = b[0:WIN, i * WIN : (i + 1) * WIN], b[WIN:, i * WIN : (i + 1) * WIN]
                    re_rows = slice(k * WIN, (k + 1) * WIN)
                    im_rows = slice(HALF + k * WIN, HALF + (k + 1) * WIN)
                    p_re, p_im = probe_now[re_rows, :], probe_now[im_rows, :]
                    g_re = g_re + p_re * b_re + p_im * b_im
                    g_im = g_im + p_re * b_im - p_im * b_re
                    w_re, w_im = win[0], win[1]
                    pg[rnd, re_rows, :] += w_re * b_re + w_im * b_im
                    pg[rnd, im_rows, :] += w_re * b_im - w_im * b_re
            turn = c & (WIN - 1)
            inside = lane >= c
            for comp, g in enumerate((g_re, g_im)):
                g = pltpu.roll(g, turn, 1)
                zp[0, comp, WIN : 2 * WIN, :] = jnp.where(inside, g, 0.0)
                zp[1, comp, WIN : 2 * WIN, :] = jnp.where(inside, 0.0, g)
            for half in range(2):
                for comp in range(2):
                    gq[rnd, half, comp] += zp[half, comp, pl.ds(WIN - r, 2 * WIN), :]
            return carry

        lax.fori_loop(0, SCANS, scan, 0)

        mine = pl.multiple_of(core * HALF, HALF)
        theirs = pl.multiple_of((1 - core) * HALF, HALF)
        core_copies = [
            remote(wacc.at[rnd], wcb.at[rnd], co_s.at[rnd, 0], co_r.at[rnd, 0], partner),
            remote(pg.at[rnd, pl.ds(theirs, HALF), :], crb.at[rnd], co_s.at[rnd, 1], co_r.at[rnd, 1], partner),
        ]
        for copy in core_copies:
            copy.start()
        lr = [
            remote(gq.at[rnd, 1], lrb.at[rnd, 0], lr_s.at[rnd, 0], lr_r.at[rnd, 0], (ty, right)),
            remote(gq.at[rnd, 0], lrb.at[rnd, 1], lr_s.at[rnd, 1], lr_r.at[rnd, 1], (ty, left)),
        ]
        for copy in lr:
            copy.start()
        for copy in core_copies:
            copy.wait_recv()
        hs[rnd] = pg[rnd, pl.ds(mine, HALF), :] + crb[rnd]
        w_pair = wacc[rnd] + wcb[rnd]
        w1[rnd, 0] = w_pair
        xy = []
        for d in range(1, X * Y):
            device, pq = xy_peer(d)
            rows = pl.ds(pl.multiple_of(pq * piece, piece), piece)
            xy.append(remote(hs.at[rnd, rows, :], rxb.at[rnd, q], xy_s.at[rnd, 0, d], xy_r.at[rnd, 0, d], device))
            xy.append(remote(w1.at[rnd, 0], wxb.at[rnd, q], xy_s.at[rnd, 1, d], xy_r.at[rnd, 1, d], device))
        for copy in xy:
            copy.start()
        for copy in lr:
            copy.wait_recv()
        eb[rnd, 0] = gq[rnd, 0] + jnp.where(has_left, lrb[rnd, 0], 0.0)
        eb[rnd, 1] = gq[rnd, 1] + jnp.where(has_right, lrb[rnd, 1], 0.0)
        ud = [
            remote(eb.at[rnd, :, :, pl.ds(128, 128), :], udb.at[rnd, 0], ud_s.at[rnd, 0], ud_r.at[rnd, 0], (down, tx)),
            remote(eb.at[rnd, :, :, pl.ds(0, 128), :], udb.at[rnd, 1], ud_s.at[rnd, 1], ud_r.at[rnd, 1], (up, tx)),
        ]
        for copy in ud:
            copy.start()
        own = pl.ds(pl.multiple_of(q * piece, piece), piece)
        rxb[rnd, q] = hs[rnd, own, :]
        wxb[rnd, q] = w_pair
        for copy in xy:
            copy.wait_recv()
        total, w_total = rxb[rnd, 0], wxb[rnd, 0]
        for i in range(1, X * Y):
            total, w_total = total + rxb[rnd, i], w_total + wxb[rnd, i]
        zbuf[rnd, z] = total
        wzb[rnd, z] = w_total
        zc = []
        for d in range(1, nz):
            device = z_peer(d)
            zc.append(remote(zbuf.at[rnd, z], zbuf.at[rnd, z], z_s.at[rnd, 0, d], z_r.at[rnd, 0, d], device))
            zc.append(remote(wzb.at[rnd, z], wzb.at[rnd, z], z_s.at[rnd, 1, d], z_r.at[rnd, 1, d], device))
        for copy in zc:
            copy.start()
        for copy in ud:
            copy.wait_recv()
        for half in range(2):
            in_cols = (lane >= 64) | has_left if half == 0 else (lane < 64) | has_right
            for row in range(2):
                rows = pl.ds(row * 128, 128)
                sub = lax.broadcasted_iota(jnp.int32, (WIN, WIN), 0)
                in_rows = (sub >= 64) | has_up if row == 0 else (sub < 64) | has_down
                there = has_up if row == 0 else has_down
                for comp in range(2):
                    add = eb[rnd, half, comp, rows, :] + jnp.where(there, udb[rnd, row, half, comp], 0.0)
                    ext[half, comp, rows, :] += jnp.where(in_cols & in_rows, OBJECT_STEP * add, 0.0)
        if rnd == ROUNDS - 1:
            for comp in range(2):
                a, b = ext[0, comp, 64:192, :], ext[1, comp, 64:192, :]
                obj_out[comp] = jnp.where(low, pltpu.roll(a, 64, 1), pltpu.roll(b, 64, 1))
        for copy in zc:
            copy.wait_recv()
        total, w_total = zbuf[rnd, 0], wzb[rnd, 0]
        for i in range(1, nz):
            total, w_total = total + zbuf[rnd, i], w_total + wzb[rnd, i]
        weight = jnp.sum(w_total, axis=(0, 1), keepdims=True)
        place = pl.ds(pl.multiple_of(core * HALF + q * piece, piece), piece)
        pn[rnd, place, :] = probe_now[place, :] + PROBE_RELAX * WIN * WIN / weight * total
        ag = []
        for d in range(1, X * Y):
            device, _ = xy_peer(d)
            ag.append(remote(pn.at[rnd, place, :], pn.at[rnd, place, :], ag_s.at[rnd, d], ag_r.at[rnd, d], device))
        for copy in ag:
            copy.start()
        fw = [remote(pn.at[rnd, place, :], pn.at[rnd, place, :], fw_s.at[rnd, 0], fw_r.at[rnd, 0], partner)]
        fw[0].start()
        for d in range(1, X * Y):
            ag[d - 1].wait_recv()
            source = ((x + X - d // Y) % X) * Y + (y + Y - d % Y) % Y
            rows = pl.ds(pl.multiple_of(core * HALF + source * piece, piece), piece)
            fw.append(remote(pn.at[rnd, rows, :], pn.at[rnd, rows, :], fw_s.at[rnd, d], fw_r.at[rnd, d], partner))
            fw[d].start()
        for copy in fw:
            copy.wait_recv()
        for copy in core_copies + lr + xy + ud + zc + ag + fw:
            copy.wait_send()
    for copy in halo:
        copy.wait_send()
    probe_out[...] = pn[ROUNDS - 1]


def per_device(object_field, probe, intensities, positions):
    nq, nz = X * Y, ZH * ZL
    piece = HALF // nq
    vmem = lambda *shape, dtype=F32: pltpu.VMEM(shape, dtype)
    dma = lambda *shape: pltpu.SemaphoreType.DMA(shape)
    r = ROUNDS
    full = pl.BlockSpec(memory_space=pltpu.VMEM)
    obj, new_probe = pl.pallas_call(
        kernel,
        out_shape=(
            jax.ShapeDtypeStruct((2, WIN, WIN), F32),
            jax.ShapeDtypeStruct((2 * HALF, WIN), F32),
        ),
        in_specs=[full, full, full, pl.BlockSpec(memory_space=pltpu.SMEM), full],
        out_specs=(full, full),
        scratch_shapes=[
            vmem(2, 2, 256, 128),
            vmem(2, 2, 384, 128),
            vmem(r, 2, 2, 256, 128),
            vmem(r, 2, 2, 256, 128),
            vmem(r, 2, 2, 256, 128),
            vmem(r, 2, 2, 2, 128, 128),
            vmem(2, 128, 128),
            vmem(2, 128, 128),
            vmem(2, 2, 64, 128),
            vmem(4, 64, 128),
            vmem(256, 512, dtype=BF16),
            vmem(256, 512, dtype=BF16),
            vmem(MODES, 128, 256),
            vmem(2, 128, 128),
            vmem(r, 2 * HALF, 128),
            vmem(r, 8, 128),
            vmem(r, HALF, 128),
            vmem(r, HALF, 128),
            vmem(r, nq, piece, 128),
            vmem(r, nz, piece, 128),
            vmem(r, 2 * HALF, 128),
            vmem(r, 8, 128),
            vmem(r, 1, 8, 128),
            vmem(r, nq, 8, 128),
            vmem(r, nz, 8, 128),
            dma(8), dma(8),
            dma(r, 2), dma(r, 2),
            dma(r, 2), dma(r, 2),
            dma(r, 2), dma(r, 2),
            dma(r, 2, nq), dma(r, 2, nq),
            dma(r, 2, nz), dma(r, 2, nz),
            dma(r, nq), dma(r, nq),
            dma(r, nq), dma(r, nq),
        ],
        compiler_params=pltpu.CompilerParams(
            collective_id=0, has_side_effects=True, vmem_limit_bytes=48 * 1024 * 1024
        ),
    )(
        object_field,
        probe.reshape(2 * HALF, WIN),
        intensities.reshape(SCANS, WIN, WIN),
        positions.reshape(SCANS, 2),
        jnp.asarray(dft_tables()),
    )
    return obj, new_probe.reshape(2, MODES, WIN, WIN)


def solution(mesh):
    placed = (P(None, "ty", "tx"), P(), P("ty", "tx", None, None, None), P("ty", "tx", None, None))
    return jax.shard_map(
        per_device,
        mesh=mesh,
        in_specs=placed,
        out_specs=(P(None, "ty", "tx"), P()),
        check_vma=False,
    )
```

time: 744 us -> 106 us (0.14); the launches traced: 733 us -> 105 us
  waiting for transfers between devices: 438 us -> 0 us
  Pallas kernels: 0 us -> 98.5 us
  blocking collectives: 93.4 us -> 0 us
  matrix products: 61.5 us -> 0 us
  starting transfers between devices: 52.4 us -> 0 us
  local copies, waits for them, and re-layouts: 33.2 us -> 6.13 us
  loops' own time: 24.5 us -> 0 us
  between operations: 17 us -> 0.65 us
  other arithmetic: 13.7 us -> 0 us
    psum x2 -> x0, waiting for transfers between devices: 399 us -> none  [per_device(): grad_total, weight_all = lax.psum((probe_grad, weight), ('ty', 'tx'))]
    pallas_call x0 -> x1, Pallas kernels: none -> 98.5 us  [per_device(): pl.pallas_call(kernel, out_shape=(jax.ShapeDtypeStruct((2, WIN, WIN), F32...]
    psum x1 -> x0, blocking collectives: 93.4 us -> none  [per_device(): grad_total, weight_all = lax.psum((probe_grad, weight), ('ty', 'tx'))]
    dot_general x32 -> x0, matrix products: 61.5 us -> none  [the longest x4 18.4 us: transform(): s_re = jnp.einsum('bxy,vy->bxv', mid_re, sine_table, precision=exact)]
    ppermute x16 -> x0, starting transfers between devices: 52.3 us -> none  [the longest x8 39.4 us: padded_2(): before = lax.ppermute(last, axis, up)]
    ppermute x16 -> x0, waiting for transfers between devices: 38.9 us -> none  [the longest x8 33.7 us: padded_2(): after = lax.ppermute(initial, axis, down)]
    another operation x4 -> x0, loops' own time: 24.5 us -> none  [the longest x2 24.3 us: per_device(): grad_grid = lax.fori_loop(0, scan_count, place, jnp.zeros_like(extended))]
    dynamic_update_slice x6 -> x0, local copies, waits for them, and re-layouts: 13.5 us -> none  [place(): lax.dynamic_update_slice(grid_now, previous + grad_piece, start_tuple)]
  transfers between devices with their start and end apart: 18 -> 0, of which waited for: 13 -> 0; matrix products, arithmetic and copies ran while one was open for 2% -> 0% of each run, Pallas kernels for 0% -> 0%
where the time goes in v1:
time: 106 us; the launch traced here: 105 us
  Pallas kernels  98.5 us (93%)
  local copies, waits for them, and re-layouts  6.13 us (6%)
    pallas_call x1, Pallas kernels, per_device(): pl.pallas_call(kernel, out_shape=(jax.ShapeDtypeStruct((2, WIN, WIN), F32...  98.5 us
    unnamed x12, local copies, waits for them, and re-layouts  6.03 us

profile of v1, /device:TPU:1, one launch (start us, length us, event | category | flops | bytes accessed | tf_op | source)
XLA Modules:
  0.0 105.3 jit_solution(16195224441104047722)
XLA Ops:
  0.6 0.0 copy-start.4
  0.6 0.7 copy-done.4
  1.3 0.1 copy.7.pos
  1.4 0.0 copy-start
  1.4 1.0 copy-done
  2.4 0.0 copy-start.1
  2.4 1.0 copy-done.1
  3.5 0.0 copy-start.2
  3.5 0.9 copy-done.2
  4.4 0.0 copy-start.3
  4.4 0.9 copy-done.3
  5.3 98.5 %shard_map.68 = (f32[2,128,128]{2,1,0:T(8,128)S(1)}, f32[1024,128]{1,0:T(8,128)S(1)}) custom-call(f32[2,128,128]{2,1,0:T(8,128)S(1)} %copy-done.3, f32[1024,128]{1,0:T(8,128)S(1)} %bitcast.4, f32[3,128,128]{2,1,0:T(8,128)S(1)} %bitcast.6, s32[3,2]{1,0:T(4,128)S(1)} %copy.7.pos, bf16[4,256,256]{2,1,0:T(8,128)(2,1)S(1)} %copy-done.1), custom_call_target="tpu_custom_call" | custom-call | tf_op jit(solution)/shard_map/pallas_call | solution.py:309
  103.8 0.7 copy.10
  104.5 0.8 copy.11
Async XLA Ops:
  0.6 0.7 copy-start.4
  1.4 1.0 copy-start
  2.4 1.0 copy-start.1
  3.5 0.9 copy-start.2
  4.4 0.9 copy-start.3

commit v2 on v0

v2 whole, which is shorter than its diff:
```python
import jax
import jax.numpy as jnp
import ml_dtypes
import numpy as np
from jax import lax
from jax.experimental import pallas as pl
from jax.experimental.pallas import tpu as pltpu
from jax.sharding import PartitionSpec as P

ROUNDS = 2
OBJECT_STEP = 0.1
PROBE_RELAX = 0.5
WIN = 128
MODES = 4
SCANS = 3
PAIRS = MODES // 2
X, Y, ZH, ZL = 4, 4, 2, 4
HALF = MODES * WIN
CHUNK = HALF // PAIRS
MESH = pl.DeviceIdType.MESH
F32, BF16 = jnp.float32, jnp.bfloat16


def dft_tables():
    line = np.arange(WIN)
    angle = (line[:, None] * line[None, :] % WIN) * (2.0 * np.pi / WIN)
    c, s = np.cos(angle) * WIN**-0.5, np.sin(angle) * WIN**-0.5
    a = np.block([[c, -s], [s, c]])
    parts = []
    for m in (a, a.T):
        hi = m.astype(ml_dtypes.bfloat16)
        lo = (m - hi.astype(np.float64)).astype(ml_dtypes.bfloat16)
        parts += [hi, lo]
    return np.stack(parts)


def split(x):
    hi = x.astype(BF16)
    return hi, (x - hi.astype(F32)).astype(BF16)


def mm(a, b):
    return jnp.dot(a, b, preferred_element_type=F32)


def left_mm(tab, i, x):
    hi, lo = split(x)
    return mm(tab[i], hi) + mm(tab[i], lo) + mm(tab[i + 1], hi)


def right_mm(x, tab, i):
    hi, lo = split(x)
    return mm(hi, tab[i]) + mm(lo, tab[i]) + mm(hi, tab[i + 1])


def regroup(t):
    top = jnp.concatenate([t[:WIN, :WIN], t[WIN:, :WIN]], axis=1)
    bottom = jnp.concatenate([t[:WIN, WIN:], t[WIN:, WIN:]], axis=1)
    return jnp.concatenate([top, bottom], axis=0)


def kernel(
    obj_hbm, probe_hbm, inten_hbm, pos, tab_hbm, obj_out, probe_out,
    probe, inten, tab, objm, hlr, pk, ext, zp, gq, lrp, lrb, mb, udb, uf, pw, win, gs, pg, wacc,
    crb, wcb, hs, rxb, zbuf, pn,
    in_s, halo_s, halo_r, lr_s, lr_r, ud_s, ud_r, co_s, co_r, xy_s, xy_r, z_s, z_r, ag_s, ag_r, fw_s, fw_r,
):
    ty, tx = lax.axis_index("ty"), lax.axis_index("tx")
    nty, ntx = ZH * X, ZL * Y * 2
    zh, x = ty // X, ty % X
    zl, y, core = tx // (2 * Y), (tx // 2) % Y, tx % 2
    z = zh * ZL + zl
    q = x * Y + y
    piece = CHUNK // (X * Y)
    nz = ZH * ZL

    has_up, has_down = ty > 0, ty < nty - 1
    has_left, has_right = tx > 0, tx < ntx - 1
    up, down = (ty + nty - 1) % nty, (ty + 1) % nty
    left, right = (tx + ntx - 1) % ntx, (tx + 1) % ntx
    partner = (ty, tx + 1 - 2 * core)

    def xy_peer(d):
        px, py = (x + d // Y) % X, (y + d % Y) % Y
        return (zh * X + px, zl * 2 * Y + py * 2 + core), px * Y + py

    def z_peer(d):
        pz = (z + d) % nz
        return ((pz // ZL) * X + x, (pz % ZL) * 2 * Y + y * 2 + core)

    def remote(src, dst, ssem, rsem, device):
        return pltpu.make_async_remote_copy(
            src_ref=src, dst_ref=dst, send_sem=ssem, recv_sem=rsem, device_id=device, device_id_type=MESH
        )

    loads = [
        pltpu.make_async_copy(obj_hbm, objm.at[0, :, pl.ds(64, WIN), :], in_s.at[0]),
        pltpu.make_async_copy(probe_hbm, probe, in_s.at[1]),
        pltpu.make_async_copy(tab_hbm, tab, in_s.at[2]),
        pltpu.make_async_copy(inten_hbm, inten, in_s.at[3]),
    ]
    for copy in loads:
        copy.start()
    peers = [partner, (ty, left), (ty, right), (up, tx), (down, tx), (up, left), (up, right), (down, left), (down, right)]
    peers += [xy_peer(d)[0] for d in range(1, X * Y)] + [z_peer(d) for d in range(1, nz)]
    barrier = pltpu.get_barrier_semaphore()
    for peer in peers:
        pl.semaphore_signal(barrier, inc=1, device_id=peer, device_id_type=MESH)

    low = lax.broadcasted_iota(jnp.int32, (WIN, WIN), 1) < 64
    lane = lax.broadcasted_iota(jnp.int32, (WIN, WIN), 1)
    low2 = lax.broadcasted_iota(jnp.int32, (2 * WIN, WIN), 1) < 64
    zp[...] = jnp.zeros_like(zp)
    loads[0].wait()

    def pack(re, im, low):
        return jnp.where(low, re, pltpu.roll(im, 64, 1)), jnp.where(low, pltpu.roll(re, 64, 1), im)

    pk[0, 0, 64:192, :], pk[0, 1, 64:192, :] = pack(objm[0, 0, 64:192, :], objm[0, 1, 64:192, :], low)

    @pl.when(jnp.logical_not(has_left))
    def _():
        hlr[:, 0] = jnp.zeros_like(hlr.at[:, 0])
        lrb[:, 0] = jnp.zeros_like(lrb.at[:, 0])

    @pl.when(jnp.logical_not(has_right))
    def _():
        hlr[:, 1] = jnp.zeros_like(hlr.at[:, 1])
        lrb[:, 1] = jnp.zeros_like(lrb.at[:, 1])

    @pl.when(jnp.logical_not(has_up))
    def _():
        hlr[0, :, 0:64, :] = jnp.zeros((2, 64, WIN), F32)
        objm[0, :, 0:64, :] = jnp.zeros((2, 64, WIN), F32)
        udb[:, 0] = jnp.zeros_like(udb.at[:, 0])

    @pl.when(jnp.logical_not(has_down))
    def _():
        hlr[0, :, 192:256, :] = jnp.zeros((2, 64, WIN), F32)
        objm[0, :, 192:256, :] = jnp.zeros((2, 64, WIN), F32)
        udb[:, 1] = jnp.zeros_like(udb.at[:, 1])

    pl.semaphore_wait(barrier, len(peers))

    def start(copies):
        for copy, to, _ in copies:
            @pl.when(to)
            def _():
                copy.start()

    def wait_recv(copies):
        for copy, _, came in copies:
            @pl.when(came)
            def _():
                copy.wait_recv()

    def wait_send(copies):
        for copy, to, _ in copies:
            @pl.when(to)
            def _():
                copy.wait_send()

    top, bottom, mid = pl.ds(64, 64), pl.ds(128, 64), pl.ds(64, 128)
    above, below = pl.ds(0, 64), pl.ds(192, 64)
    halo = [
        (objm.at[0, :, bottom, :], objm.at[0, :, above, :], (down, tx), has_down, has_up),
        (objm.at[0, :, top, :], objm.at[0, :, below, :], (up, tx), has_up, has_down),
        (pk.at[0, 1, mid, :], hlr.at[0, 0, mid, :], (ty, right), has_right, has_left),
        (pk.at[0, 0, mid, :], hlr.at[0, 1, mid, :], (ty, left), has_left, has_right),
        (pk.at[0, 1, bottom, :], hlr.at[0, 0, above, :], (down, right), has_down & has_right, has_up & has_left),
        (pk.at[0, 0, bottom, :], hlr.at[0, 1, above, :], (down, left), has_down & has_left, has_up & has_right),
        (pk.at[0, 1, top, :], hlr.at[0, 0, below, :], (up, right), has_up & has_right, has_down & has_left),
        (pk.at[0, 0, top, :], hlr.at[0, 1, below, :], (up, left), has_up & has_left, has_down & has_right),
    ]
    halo = [(remote(s, d, halo_s.at[i], halo_r.at[i], p), to, came) for i, (s, d, p, to, came) in enumerate(halo)]
    start(halo)
    for copy in loads[1:]:
        copy.wait()
    sent = [halo]
    wait_recv(halo)

    def windows(rnd):
        m_re, m_im = pltpu.roll(objm[rnd, 0], 64, 1), pltpu.roll(objm[rnd, 1], 64, 1)
        fl, fr = hlr[rnd, 0], hlr[rnd, 1]
        ext[0, 0] = jnp.where(low2, fl, m_re)
        ext[0, 1] = jnp.where(low2, pltpu.roll(fl, 64, 1), m_im)
        ext[1, 0] = jnp.where(low2, m_re, pltpu.roll(fr, 64, 1))
        ext[1, 1] = jnp.where(low2, m_im, fr)
        wacc[rnd] = jnp.zeros_like(wacc.at[rnd])
        gq[rnd] = jnp.zeros_like(gq.at[rnd])
        pg[rnd] = jnp.zeros_like(pg.at[rnd])

        def cut(s, carry):
            r, c = pos[s, 0], pos[s, 1]
            back = (WIN - c) & (WIN - 1)
            first = lane + c < WIN
            w = wacc[rnd]
            for comp in range(2):
                x0 = pltpu.roll(ext[0, comp, pl.ds(r, WIN), :], back, 1)
                x1 = pltpu.roll(ext[1, comp, pl.ds(r, WIN), :], back, 1)
                o = jnp.where(first, x0, x1)
                win[s, comp] = o
                w = w + jnp.sum((o * o).reshape(WIN // 8, 8, WIN), axis=0)
            wacc[rnd] = w
            return carry

        lax.fori_loop(0, SCANS, cut, 0, unroll=True)

    def modes_of(ref, j):
        return [
            (ref[k * WIN : (k + 1) * WIN, :], ref[HALF + k * WIN : HALF + (k + 1) * WIN, :])
            for k in range(2 * j, 2 * j + 2)
        ]

    def forward(probe_now, j):
        def step(s, carry):
            w_re, w_im = win[s, 0], win[s, 1]
            (a_re, a_im), (b_re, b_im) = modes_of(probe_now, j)
            wave_re = jnp.concatenate([a_re * w_re - a_im * w_im, b_re * w_re - b_im * w_im], axis=1)
            wave_im = jnp.concatenate([a_re * w_im + a_im * w_re, b_re * w_im + b_im * w_re], axis=1)
            t = left_mm(tab, 2, jnp.concatenate([wave_re, wave_im], axis=0))
            u = right_mm(regroup(t), tab, 0)
            uf[s, j] = u
            u2 = u * u
            p = (u2[:WIN, :WIN] + u2[:WIN, WIN:]) + (u2[WIN:, :WIN] + u2[WIN:, WIN:])
            if j == 0:
                pw[s] = p
            else:
                p = pw[s] + p
                pw[s] = jnp.sqrt(inten[s]) / jnp.sqrt(jnp.maximum(p, 1.0)) - 1.0
            return carry

        lax.fori_loop(0, SCANS, step, 0, unroll=True)

    def backward(rnd, probe_now, j, lo, hi):
        def step(s, carry):
            f = jnp.concatenate([pw[s], pw[s]], axis=1)
            b = right_mm(uf[s, j] * jnp.concatenate([f, f], axis=0), tab, 2)
            t = left_mm(tab, 0, regroup(b))
            w_re, w_im = win[s, 0], win[s, 1]
            g_re, g_im = (0.0, 0.0) if j == 0 else (gs[s, 0], gs[s, 1])
            for i, (p_re, p_im) in enumerate(modes_of(probe_now, j)):
                k = 2 * j + i
                b_re, b_im = t[:WIN, i * WIN : (i + 1) * WIN], t[WIN:, i * WIN : (i + 1) * WIN]
                g_re = g_re + p_re * b_re + p_im * b_im
                g_im = g_im + p_re * b_im - p_im * b_re
                pg[rnd, k * WIN : (k + 1) * WIN, :] += w_re * b_re + w_im * b_im
                pg[rnd, HALF + k * WIN : HALF + (k + 1) * WIN, :] += w_re * b_im - w_im * b_re
            if j < PAIRS - 1:
                gs[s, 0], gs[s, 1] = g_re, g_im
            else:
                r, c = pos[s, 0], pos[s, 1]
                turn = c & (WIN - 1)
                inside = lane >= c
                for comp, g in enumerate((g_re, g_im)):
                    g = pltpu.roll(g, turn, 1)
                    zp[0, comp, WIN : 2 * WIN, :] = jnp.where(inside, g, 0.0)
                    zp[1, comp, WIN : 2 * WIN, :] = jnp.where(inside, 0.0, g)
                for half in range(2):
                    for comp in range(2):
                        gq[rnd, half, comp] += zp[half, comp, pl.ds(WIN - r, 2 * WIN), :]
            return carry

        lax.fori_loop(lo, hi, step, 0, unroll=True)

    def all_reduce(rnd, probe_now, j):
        rows = piece + (8 if j == 0 else 0)
        n = pl.ds(0, rows)
        copies = []

        def go(new):
            for copy in new:
                copy.start()
            copies.extend(new)
            return new

        theirs = pl.ds(pl.multiple_of((1 - core) * HALF + j * CHUNK, CHUNK), CHUNK)
        new = [remote(pg.at[rnd, theirs, :], crb.at[rnd, j], co_s.at[rnd, j], co_r.at[rnd, j], partner)]
        if j == 0:
            new.append(remote(wacc.at[rnd], wcb.at[rnd], co_s.at[rnd, PAIRS], co_r.at[rnd, PAIRS], partner))
        new = go(new)
        yield
        for copy in new:
            copy.wait_recv()
        mine = pl.ds(pl.multiple_of(core * HALF + j * CHUNK, CHUNK), CHUNK)
        hs[rnd, j, :, 0:piece, :] = (pg[rnd, mine, :] + crb[rnd, j]).reshape(X * Y, piece, WIN)
        if j == 0:
            hs[rnd, j, :, piece:, :] = jnp.broadcast_to((wacc[rnd] + wcb[rnd])[None], (X * Y, 8, WIN))
        new = []
        for d in range(1, X * Y):
            device, pq = xy_peer(d)
            new.append(remote(hs.at[rnd, j, pq, n, :], rxb.at[rnd, j, q, n, :], xy_s.at[rnd, j, d], xy_r.at[rnd, j, d], device))
        new = go(new)
        rxb[rnd, j, q, 0:rows, :] = hs[rnd, j, q, 0:rows, :]
        yield
        for copy in new:
            copy.wait_recv()
        total = rxb[rnd, j, 0, 0:rows, :]
        for i in range(1, X * Y):
            total = total + rxb[rnd, j, i, 0:rows, :]
        zbuf[rnd, j, z, 0:rows, :] = total
        here = zbuf.at[rnd, j, z, n, :]
        new = go([remote(here, here, z_s.at[rnd, j, d], z_r.at[rnd, j, d], z_peer(d)) for d in range(1, nz)])
        yield
        for copy in new:
            copy.wait_recv()
        total = zbuf[rnd, j, 0, 0:rows, :]
        for i in range(1, nz):
            total = total + zbuf[rnd, j, i, 0:rows, :]
        if j == 0:
            wcb[rnd] = jnp.broadcast_to(jnp.sum(total[piece:], axis=(0, 1), keepdims=True), (8, WIN))
        scale = PROBE_RELAX * WIN * WIN / wcb[rnd, 0:1, :]
        base = core * HALF + j * CHUNK
        place = pl.ds(pl.multiple_of(base + q * piece, piece), piece)
        pn[rnd, place, :] = probe_now[place, :] + scale * total[:piece]
        here = pn.at[rnd, place, :]
        new = go([remote(here, here, ag_s.at[rnd, j, d], ag_r.at[rnd, j, d], xy_peer(d)[0]) for d in range(1, X * Y)])
        yield
        forwards = []
        for dx in (0, 1, 3, 2) if X == 4 else range(X):
            for d in range(dx * Y, (dx + 1) * Y):
                if d:
                    new[d - 1].wait_recv()
            group = ((x + X - dx) % X) * Y * piece
            source = pn.at[rnd, pl.ds(pl.multiple_of(base + group, Y * piece), Y * piece), :]
            forwards += go([remote(source, source, fw_s.at[rnd, j, dx], fw_r.at[rnd, j, dx], partner)])
        yield
        for copy in forwards:
            copy.wait_recv()
        sent.append([(copy, True, True) for copy in copies])
        yield

    for rnd in range(ROUNDS):
        last = rnd == ROUNDS - 1
        probe_now = probe if rnd == 0 else pn.at[rnd - 1]
        if rnd == 0:
            windows(rnd)
            forward(probe_now, 0)
        forward(probe_now, 1)
        backward(rnd, probe_now, 0, 0, SCANS)
        chunk0, chunk1 = all_reduce(rnd, probe_now, 0), all_reduce(rnd, probe_now, 1)
        next(chunk0)
        backward(rnd, probe_now, 1, 0, SCANS - 1)
        next(chunk0)
        backward(rnd, probe_now, 1, SCANS - 1, SCANS)
        next(chunk1)
        lrp[rnd, 0], _ = pack(gq[rnd, 0, 0], gq[rnd, 0, 1], low2)
        _, lrp[rnd, 1] = pack(gq[rnd, 1, 0], gq[rnd, 1, 1], low2)
        lr = [
            (remote(lrp.at[rnd, 1], lrb.at[rnd, 0], lr_s.at[rnd, 0], lr_r.at[rnd, 0], (ty, right)), has_right, has_left),
            (remote(lrp.at[rnd, 0], lrb.at[rnd, 1], lr_s.at[rnd, 1], lr_r.at[rnd, 1], (ty, left)), has_left, has_right),
        ]
        start(lr)
        next(chunk1)
        wait_recv(lr)
        for comp in range(2):
            own = jnp.where(low2, pltpu.roll(gq[rnd, 0, comp], 64, 1), pltpu.roll(gq[rnd, 1, comp], 64, 1))
            a, b = lrb[rnd, 0], lrb[rnd, 1]
            if comp == 0:
                other = jnp.where(low2, a, pltpu.roll(b, 64, 1))
            else:
                other = jnp.where(low2, pltpu.roll(a, 64, 1), b)
            mb[rnd, comp] = own + other
        n = 64 if last else 128
        ud = [
            (remote(mb.at[rnd, :, pl.ds(256 - n, n), :], udb.at[rnd, 0, :, pl.ds(0, n), :], ud_s.at[rnd, 0], ud_r.at[rnd, 0], (down, tx)), has_down, has_up),
            (remote(mb.at[rnd, :, pl.ds(0, n), :], udb.at[rnd, 1, :, pl.ds(0, n), :], ud_s.at[rnd, 1], ud_r.at[rnd, 1], (up, tx)), has_up, has_down),
        ]
        start(ud)
        next(chunk0)
        next(chunk1)
        next(chunk0)
        next(chunk1)
        next(chunk0)
        next(chunk1)
        wait_recv(ud)
        if last:
            for comp in range(2):
                add = jnp.concatenate([udb[rnd, 0, comp, 0:64, :], udb[rnd, 1, comp, 0:64, :]], axis=0)
                obj_out[comp] = objm[rnd, comp, 64:192, :] + OBJECT_STEP * (mb[rnd, comp, 64:192, :] + add)
            sent += [lr, ud]
        else:
            row = lax.broadcasted_iota(jnp.int32, (WIN, WIN), 0)
            there = ((row >= 64) | has_up, (row < 64) | has_down)
            for comp in range(2):
                for half in range(2):
                    rows = slice(half * WIN, (half + 1) * WIN)
                    add = mb[rnd, comp, rows, :] + udb[rnd, half, comp]
                    objm[rnd + 1, comp, rows, :] = objm[rnd, comp, rows, :] + jnp.where(there[half], OBJECT_STEP * add, 0.0)
            pk[rnd + 1, 0], pk[rnd + 1, 1] = pack(objm[rnd + 1, 0], objm[rnd + 1, 1], low2)
            side = [
                (remote(pk.at[rnd + 1, 1], hlr.at[rnd + 1, 0], halo_s.at[8 + 2 * rnd], halo_r.at[8 + 2 * rnd], (ty, right)), has_right, has_left),
                (remote(pk.at[rnd + 1, 0], hlr.at[rnd + 1, 1], halo_s.at[9 + 2 * rnd], halo_r.at[9 + 2 * rnd], (ty, left)), has_left, has_right),
            ]
            start(side)
            sent += [lr, ud, side]
        next(chunk0)
        if not last:
            wait_recv(side)
            windows(rnd + 1)
            forward(pn.at[rnd], 0)
        next(chunk1)
    for copies in sent:
        wait_send(copies)
    probe_out[...] = pn[ROUNDS - 1]


def per_device(object_field, probe, intensities, positions):
    nq, nz = X * Y, ZH * ZL
    slot = CHUNK // nq + 8
    vmem = lambda *shape, dtype=F32: pltpu.VMEM(shape, dtype)
    dma = lambda *shape: pltpu.SemaphoreType.DMA(shape)
    r = ROUNDS
    full = pl.BlockSpec(memory_space=pltpu.VMEM)
    hbm = pl.BlockSpec(memory_space=pltpu.MemorySpace.HBM)
    obj, new_probe = pl.pallas_call(
        kernel,
        out_shape=(
            jax.ShapeDtypeStruct((2, WIN, WIN), F32),
            jax.ShapeDtypeStruct((2 * HALF, WIN), F32),
        ),
        in_specs=[hbm, hbm, hbm, pl.BlockSpec(memory_space=pltpu.SMEM), hbm],
        out_specs=(full, full),
        scratch_shapes=[
            vmem(2 * HALF, WIN),
            vmem(SCANS, WIN, WIN),
            vmem(4, 256, 256, dtype=BF16),
            vmem(r, 2, 256, 128),
            vmem(r, 2, 256, 128),
            vmem(r, 2, 256, 128),
            vmem(2, 2, 256, 128),
            vmem(2, 2, 384, 128),
            vmem(r, 2, 2, 256, 128),
            vmem(r, 2, 256, 128),
            vmem(r, 2, 256, 128),
            vmem(r, 2, 256, 128),
            vmem(r, 2, 2, 128, 128),
            vmem(SCANS, PAIRS, 256, 256),
            vmem(SCANS, 128, 128),
            vmem(SCANS, 2, 128, 128),
            vmem(SCANS, 2, 128, 128),
            vmem(r, 2 * HALF, 128),
            vmem(r, 8, 128),
            vmem(r, PAIRS, CHUNK, 128),
            vmem(r, 8, 128),
            vmem(r, PAIRS, nq, slot, 128),
            vmem(r, PAIRS, nq, slot, 128),
            vmem(r, PAIRS, nz, slot, 128),
            vmem(r, 2 * HALF, 128),
            dma(4),
            dma(8 + 2 * r), dma(8 + 2 * r),
            dma(r, 2), dma(r, 2),
            dma(r, 2), dma(r, 2),
            dma(r, PAIRS + 1), dma(r, PAIRS + 1),
            dma(r, PAIRS, nq), dma(r, PAIRS, nq),
            dma(r, PAIRS, nz), dma(r, PAIRS, nz),
            dma(r, PAIRS, nq), dma(r, PAIRS, nq),
            dma(r, PAIRS, X), dma(r, PAIRS, X),
        ],
        compiler_params=pltpu.CompilerParams(
            collective_id=0, has_side_effects=True, vmem_limit_bytes=66_000_000
        ),
    )(
        object_field,
        probe.reshape(2 * HALF, WIN),
        intensities.reshape(SCANS, WIN, WIN),
        positions.reshape(SCANS, 2),
        jnp.asarray(dft_tables()),
    )
    return obj, new_probe.reshape(2, MODES, WIN, WIN)


def solution(mesh):
    placed = (P(None, "ty", "tx"), P(), P("ty", "tx", None, None, None), P("ty", "tx", None, None))
    return jax.shard_map(
        per_device,
        mesh=mesh,
        in_specs=placed,
        out_specs=(P(None, "ty", "tx"), P()),
        check_vma=False,
    )
```

time: 744 us -> 88.6 us (0.12); the launches traced: 733 us -> 88.4 us
  waiting for transfers between devices: 438 us -> 0 us
  blocking collectives: 93.4 us -> 0 us
  Pallas kernels: 0 us -> 82.9 us
  matrix products: 61.5 us -> 0 us
  starting transfers between devices: 52.4 us -> 0 us
  local copies, waits for them, and re-layouts: 33.2 us -> 4.77 us
  loops' own time: 24.5 us -> 0 us
  between operations: 17 us -> 0.65 us
  other arithmetic: 13.7 us -> 0 us
    psum x2 -> x0, waiting for transfers between devices: 399 us -> none  [per_device(): grad_total, weight_all = lax.psum((probe_grad, weight), ('ty', 'tx'))]
    psum x1 -> x0, blocking collectives: 93.4 us -> none  [per_device(): grad_total, weight_all = lax.psum((probe_grad, weight), ('ty', 'tx'))]
    pallas_call x0 -> x1, Pallas kernels: none -> 82.9 us  [per_device(): pl.pallas_call(kernel, out_shape=(jax.ShapeDtypeStruct((2, WIN, WIN), F32...]
    dot_general x32 -> x0, matrix products: 61.5 us -> none  [the longest x4 18.4 us: transform(): s_re = jnp.einsum('bxy,vy->bxv', mid_re, sine_table, precision=exact)]
    ppermute x16 -> x0, starting transfers between devices: 52.3 us -> none  [the longest x8 39.4 us: padded_2(): before = lax.ppermute(last, axis, up)]
    ppermute x16 -> x0, waiting for transfers between devices: 38.9 us -> none  [the longest x8 33.7 us: padded_2(): after = lax.ppermute(initial, axis, down)]
    another operation x4 -> x0, loops' own time: 24.5 us -> none  [the longest x2 24.3 us: per_device(): grad_grid = lax.fori_loop(0, scan_count, place, jnp.zeros_like(extended))]
    dynamic_update_slice x6 -> x0, local copies, waits for them, and re-layouts: 13.5 us -> none  [place(): lax.dynamic_update_slice(grid_now, previous + grad_piece, start_tuple)]
  transfers between devices with their start and end apart: 18 -> 0, of which waited for: 13 -> 0; matrix products, arithmetic and copies ran while one was open for 2% -> 0% of each run, Pallas kernels for 0% -> 0%
where the time goes in v2:
time: 88.6 us; the launch traced here: 88.4 us
  Pallas kernels  82.9 us (94%)
  local copies, waits for them, and re-layouts  4.77 us (5%)
    pallas_call x1, Pallas kernels, per_device(): pl.pallas_call(kernel, out_shape=(jax.ShapeDtypeStruct((2, WIN, WIN), F32...  82.9 us
    unnamed x4, local copies, waits for them, and re-layouts  4.11 us

profile of v2, /device:TPU:1, one launch (start us, length us, event | category | flops | bytes accessed | tf_op | source)
XLA Modules:
  0.0 88.4 jit_solution(6106685114895309413)
XLA Ops:
  0.6 0.0 copy-start
  0.6 0.7 copy-done
  1.3 0.7 copy.7.pos
  2.0 82.9 %shard_map.68 = (f32[2,128,128]{2,1,0:T(8,128)}, f32[1024,128]{1,0:T(8,128)}) custom-call(f32[2,128,128]{2,1,0:T(8,128)} %obj_hbm.1, f32[1024,128]{1,0:T(8,128)} %bitcast.4, f32[3,128,128]{2,1,0:T(8,128)} %bitcast.6, s32[3,2]{1,0:T(4,128)} %copy.7.pos, bf16[4,256,256]{2,1,0:T(8,128)(2,1)} %constant.2.clone.tab_hbm), custom_call_target="tpu_custom_call" | custom-call | tf_op jit(solution)/shard_map/pallas_call | solution.py:416
  84.9 1.6 %copy.10 = f32[2,128,128]{2,1,0:T(8,128)} copy(f32[2,128,128]{2,1,0:T(8,128)} %get-tuple-element.8) | data formatting | bytes 262144
  86.5 1.9 %copy.11 = f32[2,4,128,128]{3,2,1,0:T(8,128)} copy(f32[2,4,128,128]{3,2,1,0:T(8,128)} %bitcast.5) | data formatting | bytes 1048576
Async XLA Ops:
  0.6 0.7 copy-start

commit v3 on v2

--- a/solution.py
+++ b/solution.py
@@ -18,6 +18,9 @@
 HALF = MODES * WIN
 CHUNK = HALF // PAIRS
 MESH = pl.DeviceIdType.MESH
+MIDDLE = ""
+FIRST = "10o101o01o010o"
+LAST = "10o101o01o0101"
 F32, BF16 = jnp.float32, jnp.bfloat16
 
 
@@ -87,6 +90,10 @@
     def z_peer(d):
         pz = (z + d) % nz
         return ((pz // ZL) * X + x, (pz % ZL) * 2 * Y + y * 2 + core)
+
+    ring = lambda d, n: min(d, n - d)
+    far_xy = sorted(range(X * Y - 1), key=lambda i: -ring((i + 1) // Y, X) - ring((i + 1) % Y, Y))
+    far_z = sorted(range(nz - 1), key=lambda i: -ring(i + 1, nz))
 
     def remote(src, dst, ssem, rsem, device):
         return pltpu.make_async_remote_copy(
@@ -191,7 +198,7 @@
         pg[rnd] = jnp.zeros_like(pg.at[rnd])
 
         def cut(s, carry):
-            r, c = pos[s, 0], pos[s, 1]
+            r, c = pos[0, s], pos[1, s]
             back = (WIN - c) & (WIN - 1)
             first = lane + c < WIN
             w = wacc[rnd]
@@ -249,7 +256,7 @@
             if j < PAIRS - 1:
                 gs[s, 0], gs[s, 1] = g_re, g_im
             else:
-                r, c = pos[s, 0], pos[s, 1]
+                r, c = pos[0, s], pos[1, s]
                 turn = c & (WIN - 1)
                 inside = lane >= c
                 for comp, g in enumerate((g_re, g_im)):
@@ -268,9 +275,9 @@
         n = pl.ds(0, rows)
         copies = []
 
-        def go(new):
-            for copy in new:
-                copy.start()
+        def go(new, order=None):
+            for i in order or range(len(new)):
+                new[i].start()
             copies.extend(new)
             return new
 
@@ -290,7 +297,7 @@
         for d in range(1, X * Y):
             device, pq = xy_peer(d)
             new.append(remote(hs.at[rnd, j, pq, n, :], rxb.at[rnd, j, q, n, :], xy_s.at[rnd, j, d], xy_r.at[rnd, j, d], device))
-        new = go(new)
+        new = go(new, far_xy)
         rxb[rnd, j, q, 0:rows, :] = hs[rnd, j, q, 0:rows, :]
         yield
         for copy in new:
@@ -300,7 +307,7 @@
             total = total + rxb[rnd, j, i, 0:rows, :]
         zbuf[rnd, j, z, 0:rows, :] = total
         here = zbuf.at[rnd, j, z, n, :]
-        new = go([remote(here, here, z_s.at[rnd, j, d], z_r.at[rnd, j, d], z_peer(d)) for d in range(1, nz)])
+        new = go([remote(here, here, z_s.at[rnd, j, d], z_r.at[rnd, j, d], z_peer(d)) for d in range(1, nz)], far_z)
         yield
         for copy in new:
             copy.wait_recv()
@@ -314,7 +321,7 @@
         place = pl.ds(pl.multiple_of(base + q * piece, piece), piece)
         pn[rnd, place, :] = probe_now[place, :] + scale * total[:piece]
         here = pn.at[rnd, place, :]
-        new = go([remote(here, here, ag_s.at[rnd, j, d], ag_r.at[rnd, j, d], xy_peer(d)[0]) for d in range(1, X * Y)])
+        new = go([remote(here, here, ag_s.at[rnd, j, d], ag_r.at[rnd, j, d], xy_peer(d)[0]) for d in range(1, X * Y)], far_xy)
         yield
         forwards = []
         for dx in (0, 1, 3, 2) if X == 4 else range(X):
@@ -330,6 +337,54 @@
         sent.append([(copy, True, True) for copy in copies])
         yield
 
+    def object_exchange(rnd, last):
+        lrp[rnd, 0], _ = pack(gq[rnd, 0, 0], gq[rnd, 0, 1], low2)
+        _, lrp[rnd, 1] = pack(gq[rnd, 1, 0], gq[rnd, 1, 1], low2)
+        lr = [
+            (remote(lrp.at[rnd, 1], lrb.at[rnd, 0], lr_s.at[rnd, 0], lr_r.at[rnd, 0], (ty, right)), has_right, has_left),
+            (remote(lrp.at[rnd, 0], lrb.at[rnd, 1], lr_s.at[rnd, 1], lr_r.at[rnd, 1], (ty, left)), has_left, has_right),
+        ]
+        start(lr)
+        yield
+        wait_recv(lr)
+        a, b = lrb[rnd, 0], lrb[rnd, 1]
+        others = (jnp.where(low2, a, pltpu.roll(b, 64, 1)), jnp.where(low2, pltpu.roll(a, 64, 1), b))
+        for comp, other in enumerate(others):
+            own = jnp.where(low2, pltpu.roll(gq[rnd, 0, comp], 64, 1), pltpu.roll(gq[rnd, 1, comp], 64, 1))
+            mb[rnd, comp] = own + other
+        n = 64 if last else 128
+        ud = [
+            (remote(mb.at[rnd, :, pl.ds(256 - n, n), :], udb.at[rnd, 0, :, pl.ds(0, n), :], ud_s.at[rnd, 0], ud_r.at[rnd, 0], (down, tx)), has_down, has_up),
+            (remote(mb.at[rnd, :, pl.ds(0, n), :], udb.at[rnd, 1, :, pl.ds(0, n), :], ud_s.at[rnd, 1], ud_r.at[rnd, 1], (up, tx)), has_up, has_down),
+        ]
+        start(ud)
+        sent.extend([lr, ud])
+        yield
+        wait_recv(ud)
+        if last:
+            for comp in range(2):
+                add = jnp.concatenate([udb[rnd, 0, comp, 0:64, :], udb[rnd, 1, comp, 0:64, :]], axis=0)
+                obj_out[comp] = objm[rnd, comp, 64:192, :] + OBJECT_STEP * (mb[rnd, comp, 64:192, :] + add)
+            yield
+            return
+        row = lax.broadcasted_iota(jnp.int32, (WIN, WIN), 0)
+        there = ((row >= 64) | has_up, (row < 64) | has_down)
+        for comp in range(2):
+            for half in range(2):
+                rows = slice(half * WIN, (half + 1) * WIN)
+                add = mb[rnd, comp, rows, :] + udb[rnd, half, comp]
+                objm[rnd + 1, comp, rows, :] = objm[rnd, comp, rows, :] + jnp.where(there[half], OBJECT_STEP * add, 0.0)
+        pk[rnd + 1, 0], pk[rnd + 1, 1] = pack(objm[rnd + 1, 0], objm[rnd + 1, 1], low2)
+        side = [
+            (remote(pk.at[rnd + 1, 1], hlr.at[rnd + 1, 0], halo_s.at[8 + 2 * rnd], halo_r.at[8 + 2 * rnd], (ty, right)), has_right, has_left),
+            (remote(pk.at[rnd + 1, 0], hlr.at[rnd + 1, 1], halo_s.at[9 + 2 * rnd], halo_r.at[9 + 2 * rnd], (ty, left)), has_left, has_right),
+        ]
+        start(side)
+        sent.append(side)
+        yield
+        wait_recv(side)
+        yield
+
     for rnd in range(ROUNDS):
         last = rnd == ROUNDS - 1
         probe_now = probe if rnd == 0 else pn.at[rnd - 1]
@@ -337,69 +392,24 @@
             windows(rnd)
             forward(probe_now, 0)
         forward(probe_now, 1)
+        steps = {"0": all_reduce(rnd, probe_now, 0), "1": all_reduce(rnd, probe_now, 1), "o": object_exchange(rnd, last)}
+
+        def do(order):
+            for name in order:
+                next(steps[name])
+
         backward(rnd, probe_now, 0, 0, SCANS)
-        chunk0, chunk1 = all_reduce(rnd, probe_now, 0), all_reduce(rnd, probe_now, 1)
-        next(chunk0)
+        do("0")
         backward(rnd, probe_now, 1, 0, SCANS - 1)
-        next(chunk0)
+        do(MIDDLE)
         backward(rnd, probe_now, 1, SCANS - 1, SCANS)
-        next(chunk1)
-        lrp[rnd, 0], _ = pack(gq[rnd, 0, 0], gq[rnd, 0, 1], low2)
-        _, lrp[rnd, 1] = pack(gq[rnd, 1, 0], gq[rnd, 1, 1], low2)
-        lr = [
-            (remote(lrp.at[rnd, 1], lrb.at[rnd, 0], lr_s.at[rnd, 0], lr_r.at[rnd, 0], (ty, right)), has_right, has_left),
-            (remote(lrp.at[rnd, 0], lrb.at[rnd, 1], lr_s.at[rnd, 1], lr_r.at[rnd, 1], (ty, left)), has_left, has_right),
-        ]
-        start(lr)
-        next(chunk1)
-        wait_recv(lr)
-        for comp in range(2):
-            own = jnp.where(low2, pltpu.roll(gq[rnd, 0, comp], 64, 1), pltpu.roll(gq[rnd, 1, comp], 64, 1))
-            a, b = lrb[rnd, 0], lrb[rnd, 1]
-            if comp == 0:
-                other = jnp.where(low2, a, pltpu.roll(b, 64, 1))
-            else:
-                other = jnp.where(low2, pltpu.roll(a, 64, 1), b)
-            mb[rnd, comp] = own + other
-        n = 64 if last else 128
-        ud = [
-            (remote(mb.at[rnd, :, pl.ds(256 - n, n), :], udb.at[rnd, 0, :, pl.ds(0, n), :], ud_s.at[rnd, 0], ud_r.at[rnd, 0], (down, tx)), has_down, has_up),
-            (remote(mb.at[rnd, :, pl.ds(0, n), :], udb.at[rnd, 1, :, pl.ds(0, n), :], ud_s.at[rnd, 1], ud_r.at[rnd, 1], (up, tx)), has_up, has_down),
-        ]
-        start(ud)
-        next(chunk0)
-        next(chunk1)
-        next(chunk0)
-        next(chunk1)
-        next(chunk0)
-        next(chunk1)
-        wait_recv(ud)
         if last:
-            for comp in range(2):
-                add = jnp.concatenate([udb[rnd, 0, comp, 0:64, :], udb[rnd, 1, comp, 0:64, :]], axis=0)
-                obj_out[comp] = objm[rnd, comp, 64:192, :] + OBJECT_STEP * (mb[rnd, comp, 64:192, :] + add)
-            sent += [lr, ud]
+            do(LAST)
         else:
-            row = lax.broadcasted_iota(jnp.int32, (WIN, WIN), 0)
-            there = ((row >= 64) | has_up, (row < 64) | has_down)
-            for comp in range(2):
-                for half in range(2):
-                    rows = slice(half * WIN, (half + 1) * WIN)
-                    add = mb[rnd, comp, rows, :] + udb[rnd, half, comp]
-                    objm[rnd + 1, comp, rows, :] = objm[rnd, comp, rows, :] + jnp.where(there[half], OBJECT_STEP * add, 0.0)
-            pk[rnd + 1, 0], pk[rnd + 1, 1] = pack(objm[rnd + 1, 0], objm[rnd + 1, 1], low2)
-            side = [
-                (remote(pk.at[rnd + 1, 1], hlr.at[rnd + 1, 0], halo_s.at[8 + 2 * rnd], halo_r.at[8 + 2 * rnd], (ty, right)), has_right, has_left),
-                (remote(pk.at[rnd + 1, 0], hlr.at[rnd + 1, 1], halo_s.at[9 + 2 * rnd], halo_r.at[9 + 2 * rnd], (ty, left)), has_left, has_right),
-            ]
-            start(side)
-            sent += [lr, ud, side]
-        next(chunk0)
-        if not last:
-            wait_recv(side)
+            do(FIRST)
             windows(rnd + 1)
             forward(pn.at[rnd], 0)
-        next(chunk1)
+            do("1")
     for copies in sent:
         wait_send(copies)
     probe_out[...] = pn[ROUNDS - 1]
@@ -464,7 +474,7 @@
         object_field,
         probe.reshape(2 * HALF, WIN),
         intensities.reshape(SCANS, WIN, WIN),
-        positions.reshape(SCANS, 2),
+        positions.reshape(SCANS, 2).T,
         jnp.asarray(dft_tables()),
     )
     return obj, new_probe.reshape(2, MODES, WIN, WIN)

time: 88.6 us -> 80.2 us (0.905)
  Pallas kernels: 82.9 us -> 75.9 us
  local copies, waits for them, and re-layouts: 4.77 us -> 3.44 us
    pallas_call x1, Pallas kernels: 82.9 us -> 75.9 us  [per_device(): pl.pallas_call(kernel, out_shape=(jax.ShapeDtypeStruct((2, WIN, WIN), F32...]
    unnamed x4 -> x2, local copies, waits for them, and re-layouts: 4.11 us -> 3.44 us
where the time goes in v3:
time: 80.2 us; the launch traced here: 80 us
  Pallas kernels  75.9 us (95%)
  local copies, waits for them, and re-layouts  3.44 us (4%)
    pallas_call x1, Pallas kernels, per_device(): pl.pallas_call(kernel, out_shape=(jax.ShapeDtypeStruct((2, WIN, WIN), F32...  75.9 us
    unnamed x2, local copies, waits for them, and re-layouts  3.44 us

profile of v3, /device:TPU:1, one launch (start us, length us, event | category | flops | bytes accessed | tf_op | source)
XLA Modules:
  0.0 80.0 jit_solution(10463133469762636380)
XLA Ops:
  0.6 75.9 %shard_map.68 = (f32[2,128,128]{2,1,0:T(8,128)}, f32[1024,128]{1,0:T(8,128)}) custom-call(f32[2,128,128]{2,1,0:T(8,128)} %obj_hbm.1, f32[1024,128]{1,0:T(8,128)} %bitcast.6, f32[3,128,128]{2,1,0:T(8,128)} %bitcast.8, s32[2,3]{1,0:T(2,128)} %bitcast.9, bf16[4,256,256]{2,1,0:T(8,128)(2,1)} %constant.2.clone.tab_hbm), custom_call_target="tpu_custom_call" | custom-call | tf_op jit(solution)/shard_map/pallas_call | solution.py:426
  76.5 1.6 %copy.9 = f32[2,128,128]{2,1,0:T(8,128)} copy(f32[2,128,128]{2,1,0:T(8,128)} %get-tuple-element.8) | data formatting | bytes 262144
  78.1 1.9 %copy.10 = f32[2,4,128,128]{3,2,1,0:T(8,128)} copy(f32[2,4,128,128]{3,2,1,0:T(8,128)} %bitcast.7) | data formatting | bytes 1048576

commit v4 on v3

--- a/solution.py
+++ b/solution.py
@@ -18,9 +18,9 @@
 HALF = MODES * WIN
 CHUNK = HALF // PAIRS
 MESH = pl.DeviceIdType.MESH
-MIDDLE = ""
-FIRST = "10o101o01o010o"
-LAST = "10o101o01o0101"
+MIDDLE = "0"
+FIRST = "1o101o010o10o"
+LAST = "1o101o01o0101"
 F32, BF16 = jnp.float32, jnp.bfloat16
 
 
@@ -63,7 +63,7 @@
 
 
 def kernel(
-    obj_hbm, probe_hbm, inten_hbm, pos, tab_hbm, obj_out, probe_out,
+    obj_hbm, probe_hbm, inten_hbm, pos, tab_hbm, obj_hbm_out, probe_hbm_out, obj_out,
     probe, inten, tab, objm, hlr, pk, ext, zp, gq, lrp, lrb, mb, udb, uf, pw, win, gs, pg, wacc,
     crb, wcb, hs, rxb, zbuf, pn,
     in_s, halo_s, halo_r, lr_s, lr_r, ud_s, ud_r, co_s, co_r, xy_s, xy_r, z_s, z_r, ag_s, ag_r, fw_s, fw_r,
@@ -253,22 +253,26 @@
                 g_im = g_im + p_re * b_im - p_im * b_re
                 pg[rnd, k * WIN : (k + 1) * WIN, :] += w_re * b_re + w_im * b_im
                 pg[rnd, HALF + k * WIN : HALF + (k + 1) * WIN, :] += w_re * b_im - w_im * b_re
-            if j < PAIRS - 1:
-                gs[s, 0], gs[s, 1] = g_re, g_im
-            else:
-                r, c = pos[0, s], pos[1, s]
-                turn = c & (WIN - 1)
-                inside = lane >= c
-                for comp, g in enumerate((g_re, g_im)):
-                    g = pltpu.roll(g, turn, 1)
-                    zp[0, comp, WIN : 2 * WIN, :] = jnp.where(inside, g, 0.0)
-                    zp[1, comp, WIN : 2 * WIN, :] = jnp.where(inside, 0.0, g)
-                for half in range(2):
-                    for comp in range(2):
-                        gq[rnd, half, comp] += zp[half, comp, pl.ds(WIN - r, 2 * WIN), :]
+            gs[s, 0], gs[s, 1] = g_re, g_im
             return carry
 
         lax.fori_loop(lo, hi, step, 0, unroll=True)
+
+    def place(rnd):
+        def step(s, carry):
+            r, c = pos[0, s], pos[1, s]
+            turn = c & (WIN - 1)
+            inside = lane >= c
+            for comp in range(2):
+                g = pltpu.roll(gs[s, comp], turn, 1)
+                zp[0, comp, WIN : 2 * WIN, :] = jnp.where(inside, g, 0.0)
+                zp[1, comp, WIN : 2 * WIN, :] = jnp.where(inside, 0.0, g)
+            for half in range(2):
+                for comp in range(2):
+                    gq[rnd, half, comp] += zp[half, comp, pl.ds(WIN - r, 2 * WIN), :]
+            return carry
+
+        lax.fori_loop(0, SCANS, step, 0, unroll=True)
 
     def all_reduce(rnd, probe_now, j):
         rows = piece + (8 if j == 0 else 0)
@@ -337,7 +341,13 @@
         sent.append([(copy, True, True) for copy in copies])
         yield
 
+    out_copies = [
+        pltpu.make_async_copy(obj_out, obj_hbm_out, in_s.at[4]),
+        pltpu.make_async_copy(pn.at[ROUNDS - 1], probe_hbm_out, in_s.at[5]),
+    ]
+
     def object_exchange(rnd, last):
+        place(rnd)
         lrp[rnd, 0], _ = pack(gq[rnd, 0, 0], gq[rnd, 0, 1], low2)
         _, lrp[rnd, 1] = pack(gq[rnd, 1, 0], gq[rnd, 1, 1], low2)
         lr = [
@@ -365,6 +375,7 @@
             for comp in range(2):
                 add = jnp.concatenate([udb[rnd, 0, comp, 0:64, :], udb[rnd, 1, comp, 0:64, :]], axis=0)
                 obj_out[comp] = objm[rnd, comp, 64:192, :] + OBJECT_STEP * (mb[rnd, comp, 64:192, :] + add)
+            out_copies[0].start()
             yield
             return
         row = lax.broadcasted_iota(jnp.int32, (WIN, WIN), 0)
@@ -400,9 +411,12 @@
 
         backward(rnd, probe_now, 0, 0, SCANS)
         do("0")
-        backward(rnd, probe_now, 1, 0, SCANS - 1)
-        do(MIDDLE)
-        backward(rnd, probe_now, 1, SCANS - 1, SCANS)
+        if MIDDLE:
+            backward(rnd, probe_now, 1, 0, 1)
+            do(MIDDLE)
+            backward(rnd, probe_now, 1, 1, SCANS)
+        else:
+            backward(rnd, probe_now, 1, 0, SCANS)
         if last:
             do(LAST)
         else:
@@ -410,9 +424,27 @@
             windows(rnd + 1)
             forward(pn.at[rnd], 0)
             do("1")
+    out_copies[1].start()
     for copies in sent:
         wait_send(copies)
-    probe_out[...] = pn[ROUNDS - 1]
+    for copy in out_copies:
+        copy.wait()
+
+
+def deliver(obj, probe, obj_out, probe_out, a, b, in_s, out_s):
+    refs = [(obj, a, obj_out)]
+    for i in range(4):
+        rows = pl.ds(i * HALF // 2, HALF // 2)
+        refs.append((probe.at[rows, :], b.at[rows, :], probe_out.at[rows, :]))
+    loads = [pltpu.make_async_copy(x, y, in_s.at[i]) for i, (x, y, _) in enumerate(refs)]
+    stores = [pltpu.make_async_copy(y, z, out_s.at[i]) for i, (_, y, z) in enumerate(refs)]
+    for copy in loads:
+        copy.start()
+    for load, store in zip(loads, stores):
+        load.wait()
+        store.start()
+    for copy in stores:
+        copy.wait()
 
 
 def per_device(object_field, probe, intensities, positions):
@@ -421,7 +453,6 @@
     vmem = lambda *shape, dtype=F32: pltpu.VMEM(shape, dtype)
     dma = lambda *shape: pltpu.SemaphoreType.DMA(shape)
     r = ROUNDS
-    full = pl.BlockSpec(memory_space=pltpu.VMEM)
     hbm = pl.BlockSpec(memory_space=pltpu.MemorySpace.HBM)
     obj, new_probe = pl.pallas_call(
         kernel,
@@ -430,8 +461,9 @@
             jax.ShapeDtypeStruct((2 * HALF, WIN), F32),
         ),
         in_specs=[hbm, hbm, hbm, pl.BlockSpec(memory_space=pltpu.SMEM), hbm],
-        out_specs=(full, full),
+        out_specs=(hbm, hbm),
         scratch_shapes=[
+            vmem(2, WIN, WIN),
             vmem(2 * HALF, WIN),
             vmem(SCANS, WIN, WIN),
             vmem(4, 256, 256, dtype=BF16),
@@ -457,7 +489,7 @@
             vmem(r, PAIRS, nq, slot, 128),
             vmem(r, PAIRS, nz, slot, 128),
             vmem(r, 2 * HALF, 128),
-            dma(4),
+            dma(6),
             dma(8 + 2 * r), dma(8 + 2 * r),
             dma(r, 2), dma(r, 2),
             dma(r, 2), dma(r, 2),
@@ -477,6 +509,17 @@
         positions.reshape(SCANS, 2).T,
         jnp.asarray(dft_tables()),
     )
+    obj, new_probe = pl.pallas_call(
+        deliver,
+        out_shape=(
+            jax.ShapeDtypeStruct((2, WIN, WIN), F32),
+            jax.ShapeDtypeStruct((2 * HALF, WIN), F32),
+        ),
+        in_specs=[hbm, hbm],
+        out_specs=(hbm, hbm),
+        scratch_shapes=[vmem(2, WIN, WIN), vmem(2 * HALF, WIN), dma(5), dma(5)],
+        compiler_params=pltpu.CompilerParams(vmem_limit_bytes=66_000_000),
+    )(obj, new_probe)
     return obj, new_probe.reshape(2, MODES, WIN, WIN)
 
 

time: 80.2 us -> 77.7 us (0.969)
  local copies, waits for them, and re-layouts: 3.44 us -> 0 us
  Pallas kernels: 75.9 us -> 76.9 us
    unnamed x2 -> x0, local copies, waits for them, and re-layouts: 3.44 us -> none
    pallas_call x0 -> x1, Pallas kernels: none -> 1.91 us  [per_device(): pl.pallas_call(deliver, out_shape=(jax.ShapeDtypeStruct((2, WIN, WIN), F3...]
    pallas_call x1, Pallas kernels: 75.9 us -> 75 us  [per_device(): pl.pallas_call(kernel, out_shape=(jax.ShapeDtypeStruct((2, WIN, WIN), F32...]
where the time goes in v4:
time: 77.7 us; the launch traced here: 77.5 us
  Pallas kernels  76.9 us (99%)
    pallas_call x1, Pallas kernels, per_device(): pl.pallas_call(kernel, out_shape=(jax.ShapeDtypeStruct((2, WIN, WIN), F32...  75 us
    pallas_call x1, Pallas kernels, per_device(): pl.pallas_call(deliver, out_shape=(jax.ShapeDtypeStruct((2, WIN, WIN), F3...  1.91 us

profile of v4, /device:TPU:1, one launch (start us, length us, event | category | flops | bytes accessed | tf_op | source)
XLA Modules:
  0.0 77.5 jit_solution(5036730590770358179)
XLA Ops:
  0.6 75.0 %shard_map.68 = (f32[2,128,128]{2,1,0:T(8,128)}, f32[1024,128]{1,0:T(8,128)}) custom-call(f32[2,128,128]{2,1,0:T(8,128)} %obj_hbm.1, f32[1024,128]{1,0:T(8,128)} %bitcast.6, f32[3,128,128]{2,1,0:T(8,128)} %bitcast.7, s32[2,3]{1,0:T(2,128)} %bitcast.8, bf16[4,256,256]{2,1,0:T(8,128)(2,1)} %constant.2.clone.tab_hbm), custom_call_target="tpu_custom_call" | custom-call | tf_op jit(solution)/shard_map/pallas_call | solution.py:457
  75.6 1.9 %shard_map.69 = (f32[2,128,128]{2,1,0:T(8,128)}, f32[1024,128]{1,0:T(8,128)}) custom-call(f32[2,128,128]{2,1,0:T(8,128)} %get-tuple-element.6.obj, f32[1024,128]{1,0:T(8,128)} %get-tuple-element.7.probe), custom_call_target="tpu_custom_call" | custom-call | tf_op jit(solution)/shard_map/pallas_call | solution.py:512

commit v5 on v4

--- a/solution.py
+++ b/solution.py
@@ -343,8 +343,10 @@
 
     out_copies = [
         pltpu.make_async_copy(obj_out, obj_hbm_out, in_s.at[4]),
-        pltpu.make_async_copy(pn.at[ROUNDS - 1], probe_hbm_out, in_s.at[5]),
     ]
+    for i in range(2 * PAIRS):
+        rows = pl.ds((i % 2) * HALF + (i // 2) * CHUNK, CHUNK)
+        out_copies.append(pltpu.make_async_copy(pn.at[ROUNDS - 1, rows, :], probe_hbm_out.at[rows, :], in_s.at[5 + i]))
 
     def object_exchange(rnd, last):
         place(rnd)
@@ -418,13 +420,17 @@
         else:
             backward(rnd, probe_now, 1, 0, SCANS)
         if last:
-            do(LAST)
+            do(LAST[:-1])
+            out_copies[1].start()
+            out_copies[2].start()
+            do(LAST[-1])
         else:
             do(FIRST)
             windows(rnd + 1)
             forward(pn.at[rnd], 0)
             do("1")
-    out_copies[1].start()
+    out_copies[3].start()
+    out_copies[4].start()
     for copies in sent:
         wait_send(copies)
     for copy in out_copies:
@@ -489,7 +495,7 @@
             vmem(r, PAIRS, nq, slot, 128),
             vmem(r, PAIRS, nz, slot, 128),
             vmem(r, 2 * HALF, 128),
-            dma(6),
+            dma(5 + 2 * PAIRS),
             dma(8 + 2 * r), dma(8 + 2 * r),
             dma(r, 2), dma(r, 2),
             dma(r, 2), dma(r, 2),

time: 77.7 us -> 77.6 us (level)
  no operation moved by 1% of the time
where the time goes in v5:
time: 77.6 us; the launch traced here: 77.5 us
  Pallas kernels  76.8 us (99%)
    pallas_call x1, Pallas kernels, per_device(): pl.pallas_call(kernel, out_shape=(jax.ShapeDtypeStruct((2, WIN, WIN), F32...  74.9 us
    pallas_call x1, Pallas kernels, per_device(): pl.pallas_call(deliver, out_shape=(jax.ShapeDtypeStruct((2, WIN, WIN), F3...  1.91 us

profile of v5, /device:TPU:1, one launch (start us, length us, event | category | flops | bytes accessed | tf_op | source)
XLA Modules:
  0.0 77.5 jit_solution(8743155803282563460)
XLA Ops:
  0.6 74.9 %shard_map.68 = (f32[2,128,128]{2,1,0:T(8,128)}, f32[1024,128]{1,0:T(8,128)}) custom-call(f32[2,128,128]{2,1,0:T(8,128)} %obj_hbm.1, f32[1024,128]{1,0:T(8,128)} %bitcast.6, f32[3,128,128]{2,1,0:T(8,128)} %bitcast.7, s32[2,3]{1,0:T(2,128)} %bitcast.8, bf16[4,256,256]{2,1,0:T(8,128)(2,1)} %constant.2.clone.tab_hbm), custom_call_target="tpu_custom_call" | custom-call | tf_op jit(solution)/shard_map/pallas_call | solution.py:463
  75.6 1.9 %shard_map.69 = (f32[2,128,128]{2,1,0:T(8,128)}, f32[1024,128]{1,0:T(8,128)}) custom-call(f32[2,128,128]{2,1,0:T(8,128)} %get-tuple-element.6.obj, f32[1024,128]{1,0:T(8,128)} %get-tuple-element.7.probe), custom_call_target="tpu_custom_call" | custom-call | tf_op jit(solution)/shard_map/pallas_call | solution.py:518
